TPU v7x, 128 devices: a whole 4x4x4 slice. The times are simulated.
128 devices in a mesh: grp: 8 (over x, core), wide: 16 (over z, y).
Axes of the slice: x: 4, y: 4, z: 4, core: 2. Of those that a mesh axis runs over, the one named last changes fastest.
Arguments:
- amplitudes: float32 [4096, 64, 512], P(('grp', 'wide')), may hold values from -6 to 6
- integrals: float32 [8, 512, 512], P('grp'), may hold values from -0.25 to 0.25
- base_residual: float32 [128, 64, 512], P(('grp', 'wide')), may hold values from -6 to 6
- occ_gap: float32 [128, 64], P(('grp', 'wide')), may hold values from 0.5 to 4
- virt_sum: float32 [512], replicated, may hold values from 0.5 to 4
- task_amp: int32 [128, 96], P(('grp', 'wide')), may hold values from 0 to 511, as said below
- task_int: int32 [128, 96], P(('grp', 'wide')), may hold values from 0 to 7
- task_res: int32 [128, 96], P(('grp', 'wide')), may hold values from 0 to 15, as said below
- task_count: int32 [128], P(('grp', 'wide')), may hold values from 6 to 96, as said below
- res_owner: int32 [8, 16], P('grp'), may hold values from 0 to 15, as said below
- amp_label: int32 [4096], P(('grp', 'wide')), may hold values from 0 to 3
- int_label: int32 [8], replicated, may hold values from 0 to 3
Outputs:
- doubles_residual: float32 [128, 64, 512], P(('grp', 'wide'))
Inputs may be any that keep to these rules, and one draw needn't show every extreme that they name: `task_amp`: amplitude block t of a grp row is kept by the device of wide index t // 32 of that row, at its local position t % 32. Among the used slots of one device at most 6 name blocks kept by one device. `task_res`: among the used slots of one device at most 6 name tiles whose position (see res_owner) lies on one device. Slots from task_count on are unused; their entries are arbitrary values within the stated ranges. `res_owner`: each row is a permutation; position p of a grp row lies on the device of wide index p, at its local position p % 1.
All inputs are finite; a program needn't handle non-finite values.
Results may differ from a plain program's by a relative error of at most 0.0001.
Values sent between devices are 32-bit elements; how exact they have to be, the bound alone decides.
A program may use at most 128 MiB of HBM per device.

v0:
```python
import jax
import jax.numpy as jnp
from jax import lax
from jax.sharding import PartitionSpec as P


def bucket_ranks(holder, usable, lane_count):
    owner_hits = ((holder[:, None] == jnp.arange(lane_count)[None, :]) & usable[:, None]).astype(
        jnp.int32
    )
    before = jnp.cumsum(owner_hits, axis=0) - owner_hits
    return jnp.sum(before * owner_hits, axis=1)


def run_tasks(tile_source, tile_index, all_integrals, int_ids, signs, slot_count):
    slot_index = jnp.arange(slot_count, dtype=jnp.int32)

    def block_product(task_block):
        tiles_here = jnp.take(tile_source, tile_index[task_block], axis=0)
        weights_here = jnp.take(all_integrals, int_ids[task_block], axis=0)
        product = jnp.einsum(
            "kij,kjl->kil", tiles_here, weights_here, precision=lax.Precision.HIGHEST
        )
        return product * signs[task_block][:, None, None]

    result = lax.map(block_product, slot_index.reshape(-1, 8))
    return result.reshape(slot_count, result.shape[2], result.shape[3])


def on_device(
    amplitudes,
    integrals,
    base_residual,
    occ_gap,
    virt_sum,
    task_amp,
    task_int,
    task_res,
    task_count,
    res_owner,
    amp_label,
    int_label,
):
    lane_count = lax.axis_size("wide")
    amp_dev = amplitudes.shape[0]
    res_dev = base_residual.shape[0]
    tile_rows = amplitudes.shape[1]
    block_cols = amplitudes.shape[2]
    window = base_residual.shape[2]
    slot_count = task_amp.shape[1]
    bucket = slot_count // lane_count
    all_integrals = lax.all_gather(integrals, "grp", axis=0, tiled=True)
    slot_index = jnp.arange(slot_count, dtype=jnp.int32)
    where_kept = jnp.argsort(res_owner[0])
    usable = slot_index < task_count[0]
    tile_ids = task_amp[0]
    amp_holder = tile_ids // amp_dev
    fetch_rank = bucket_ranks(amp_holder, usable, lane_count)
    fetch_slot = jnp.where(usable, amp_holder * bucket + fetch_rank, lane_count * bucket)
    requests = (
        jnp.zeros((lane_count * bucket,), jnp.int32)
        .at[fetch_slot]
        .set(tile_ids % amp_dev, mode="drop")
    )
    incoming = lax.all_to_all(
        requests.reshape(lane_count, bucket), "wide", split_axis=0, concat_axis=0, tiled=True
    )
    asked_tiles = jnp.take(amplitudes, incoming, axis=0)
    asked_labels = jnp.take(amp_label, incoming, axis=0)
    fetched, fetched_label = (
        lax.all_to_all(asked_tiles, "wide", split_axis=0, concat_axis=0, tiled=True),
        lax.all_to_all(asked_labels, "wide", split_axis=0, concat_axis=0, tiled=True),
    )
    fetched_flat = fetched.reshape(lane_count * bucket, tile_rows, block_cols)
    read_slot = jnp.minimum(fetch_slot, lane_count * bucket - 1)
    tile_label = jnp.take(fetched_label.reshape(-1), read_slot, axis=0)
    int_ids = task_int[0]
    parity = (tile_label + jnp.take(int_label, int_ids, axis=0)) % 2
    signs = jnp.where(usable, 1.0 - 2.0 * parity.astype(jnp.float32), 0.0)
    contribution = run_tasks(fetched_flat, read_slot, all_integrals, int_ids, signs, slot_count)
    res_pos = jnp.take(where_kept, task_res[0], axis=0)
    res_dest = res_pos // res_dev
    res_local = res_pos % res_dev
    send_rank = bucket_ranks(res_dest, usable, lane_count)
    send_slot = jnp.where(usable, res_dest * bucket + send_rank, lane_count * bucket)
    outgoing = (
        jnp.zeros((lane_count * bucket, tile_rows, window), jnp.float32)
        .at[send_slot]
        .set(contribution, mode="drop")
    )
    outgoing_local = (
        jnp.full((lane_count * bucket,), res_dev, jnp.int32)
        .at[send_slot]
        .set(res_local, mode="drop")
    )
    arrived, arrived_local = (
        lax.all_to_all(
            outgoing.reshape(lane_count, bucket, tile_rows, window),
            "wide",
            split_axis=0,
            concat_axis=0,
            tiled=True,
        ),
        lax.all_to_all(
            outgoing_local.reshape(lane_count, bucket),
            "wide",
            split_axis=0,
            concat_axis=0,
            tiled=True,
        ),
    )
    select_own = (arrived_local.reshape(-1)[:, None] == jnp.arange(res_dev)[None, :]).astype(
        jnp.float32
    )
    summed = jnp.einsum(
        "nr,nx->rx",
        select_own,
        arrived.reshape(lane_count * bucket, tile_rows * window),
        precision=lax.Precision.HIGHEST,
    )
    summed = summed.reshape(res_dev, tile_rows, window)
    divisor = occ_gap[:, :, None] + virt_sum[None, None, :]
    return (base_residual + summed) / divisor


def solution(mesh):
    return jax.shard_map(
        on_device,
        mesh=mesh,
        in_specs=(
            P(("grp", "wide"), None, None),
            P("grp", None, None),
            P(("grp", "wide"), None, None),
            P(("grp", "wide"), None),
            P(),
            P(("grp", "wide"), None),
            P(("grp", "wide"), None),
            P(("grp", "wide"), None),
            P(("grp", "wide")),
            P("grp", None),
            P(("grp", "wide")),
            P(),
        ),
        out_specs=P(("grp", "wide"), None, None),
        check_vma=False,
    )
```

profile of v0, /device:TPU:0, one launch (start us, length us, event | category | flops | bytes accessed | tf_op | source)
XLA Modules:
  0.0 788.3 jit_solution(2732456752862623658)
XLA Ops:
  6.5 0.7 all-gather.2.cloned.1.call-update
  7.9 1.9 sort.17
  9.8 0.7 fusion.44
  10.5 10.6 %and_select_fusion.4 = (s32[96]{0:T(128)S(1)}, s32[96]{0:T(128)S(1)}, s32[96]{0:T(128)S(1)}, s32[96]{0:T(128)S(1)}) fusion(s32[1,96]{1,0:T(1,128)} %param.19, s32[]{:T(128)} %bitcast.34, s32[]{:T(128)} %bitcast.33, s32[]{:T(128)} %bitcast.32, s32[]{:T(128)} %bitcast.31, s32[]{:T(128)} %bitcast.30, s32[]{:T(128)} %bitcast.29, s32[]{:T(128)} %bitcast.28, ...), kind=kLoop, calls=%fused_computation.93 | loop fusion | flops 5664 | bytes 2368 | tf_op jit(solution)/shard_map/jit(remainder)/select_n | solution.py:63
  21.7 0.7 fusion.38
  22.4 0.9 scatter_custom_fusion.1
  23.3 15.5 %all_to_all.40 = s32[16,1,6]{2,1,0:T(1,128)S(1)} all-to-all(s32[16,1,6]{2,1,0:T(1,128)S(1)} %bitcast.220), channel_id=1, replica_groups=mesh['grp'=8,'wide'=16] {'wide'}, dimensions={0} | all-to-all | bytes 768 | tf_op jit(solution)/shard_map/all_to_all | solution.py:65
  39.3 11.1 %gather_fusion.5 = f32[96,64,512]{2,1,0:T(8,128)} fusion(f32[32,64,512]{2,1,0:T(8,128)} %param.14, s32[1024]{0:T(1024)S(1)} %pad_clamp_fusion.4), kind=kCustom, calls=%fused_computation.5 | custom fusion | bytes 25166208 | tf_op jit(solution)/shard_map/jit(_take)/gather | solution.py:68
  50.4 1.2 gather_fusion.6
  52.3 3.5 all-to-all-start.3
  55.8 12.3 %broadcast_select_fusion = f32[16,6,64,512]{3,2,1,0:T(8,128)} fusion(f32[16,6,64,512]{3,2,1,0:T(8,128)} %bitcast.216, pred[16,6]{1,0:T(8,128)(4,1)S(1)} %copy.25), kind=kLoop, calls=%fused_computation.38 | loop fusion | flops 3145728 | bytes 25165920 | tf_op jit(solution)/shard_map/jit(_take)/select_n | solution.py:68
  68.1 7.3 all-to-all-start.2
  75.5 0.9 scatter_custom_fusion
  76.4 0.7 all_to_all.26
  77.1 0.7 fusion.43
  79.0 1.2 gather_fusion.7
  80.2 5.0 fusion.32
  85.2 171.6 %all-to-all-done.2 = f32[16,6,64,512]{3,2,1,0:T(8,128)} async-done(((f32[16,6,64,512]{3,2,1,0:T(8,128)}), f32[16,6,64,512]{3,2,1,0:T(8,128)}, u32[]{:S(2)}, u32[]{:S(2)}) %all-to-all-start.2) | async-done | bytes 12582944 | tf_op jit(solution)/shard_map/all_to_all | solution.py:71
  256.8 6.1 all-to-all-start
  262.9 286.2 %while.10 = (s32[]{:T(128)}, f32[12,8,64,512]{3,2,1,0:T(8,128)}, s32[12,8]{1,0:T(8,128)S(1)}, s32[96]{0:T(128)S(1)}, f32[96,64,512]{2,1,0:T(8,128)}, /*index=5*/...) while((s32[]{:T(128)}, f32[12,8,64,512]{3,2,1,0:T(8,128)}, s32[12,8]{1,0:T(8,128)S(1)}, ...), condition=%wide.region_8.9_spmd, body=%wide.region_7.8_spmd.sunk | while | flops 1613237376 | bytes 29373792 | solution.py:26
  263.6 0.6 gather_fusion.1
  264.3 7.7 gather_fusion.2
  271.9 5.2 gather_fusion.3
  277.8 9.0 %fusion.55 = f32[12,8,64,512]{3,2,1,0:T(8,128)} fusion(f32[12,8,64,512]{3,2,1,0:T(8,128)} %get-tuple-element.175, s32[]{:T(128)} %get-tuple-element.174, f32[8,512,512]{2,1,0:T(8,128)} %gather_fusion.2, pred[8]{0:T(512)(128)(4,1)S(1)} %get-tuple-element.162, f32[8,64,512]{2,1,0:T(8,128)S(1)} %gather_fusion.3, f32[8]{0:T(128)S(1)} %gather_fusion.4, ...), kind=kOutput, calls=%fused_computation.17.clone.1 | convolution fusion | flops 1613234176 | bytes 10486320 | tf_op jit(solution)/shard_map/while/body/eval_jaxpr/kij,kjl->kil/dot_general | solution.py:21
  287.5 0.6 gather_fusion.1
  288.1 7.7 gather_fusion.2
  295.8 5.2 gather_fusion.3
  301.7 9.0 %fusion.55 = f32[12,8,64,512]{3,2,1,0:T(8,128)} fusion(f32[12,8,64,512]{3,2,1,0:T(8,128)} %get-tuple-element.175, s32[]{:T(128)} %get-tuple-element.174, f32[8,512,512]{2,1,0:T(8,128)} %gather_fusion.2, pred[8]{0:T(512)(128)(4,1)S(1)} %get-tuple-element.162, f32[8,64,512]{2,1,0:T(8,128)S(1)} %gather_fusion.3, f32[8]{0:T(128)S(1)} %gather_fusion.4, ...), kind=kOutput, calls=%fused_computation.17.clone.1 | convolution fusion | flops 1613234176 | bytes 10486320 | tf_op jit(solution)/shard_map/while/body/eval_jaxpr/kij,kjl->kil/dot_general | solution.py:21
  312.0 7.7 gather_fusion.2
  319.6 5.2 gather_fusion.3
  325.5 9.0 %fusion.55 = f32[12,8,64,512]{3,2,1,0:T(8,128)} fusion(f32[12,8,64,512]{3,2,1,0:T(8,128)} %get-tuple-element.175, s32[]{:T(128)} %get-tuple-element.174, f32[8,512,512]{2,1,0:T(8,128)} %gather_fusion.2, pred[8]{0:T(512)(128)(4,1)S(1)} %get-tuple-element.162, f32[8,64,512]{2,1,0:T(8,128)S(1)} %gather_fusion.3, f32[8]{0:T(128)S(1)} %gather_fusion.4, ...), kind=kOutput, calls=%fused_computation.17.clone.1 | convolution fusion | flops 1613234176 | bytes 10486320 | tf_op jit(solution)/shard_map/while/body/eval_jaxpr/kij,kjl->kil/dot_general | solution.py:21
  335.8 7.7 gather_fusion.2
  343.5 5.2 gather_fusion.3
  349.3 9.0 %fusion.55 = f32[12,8,64,512]{3,2,1,0:T(8,128)} fusion(f32[12,8,64,512]{3,2,1,0:T(8,128)} %get-tuple-element.175, s32[]{:T(128)} %get-tuple-element.174, f32[8,512,512]{2,1,0:T(8,128)} %gather_fusion.2, pred[8]{0:T(512)(128)(4,1)S(1)} %get-tuple-element.162, f32[8,64,512]{2,1,0:T(8,128)S(1)} %gather_fusion.3, f32[8]{0:T(128)S(1)} %gather_fusion.4, ...), kind=kOutput, calls=%fused_computation.17.clone.1 | convolution fusion | flops 1613234176 | bytes 10486320 | tf_op jit(solution)/shard_map/while/body/eval_jaxpr/kij,kjl->kil/dot_general | solution.py:21
  359.6 7.7 gather_fusion.2
  367.3 5.2 gather_fusion.3
  373.2 9.0 %fusion.55 = f32[12,8,64,512]{3,2,1,0:T(8,128)} fusion(f32[12,8,64,512]{3,2,1,0:T(8,128)} %get-tuple-element.175, s32[]{:T(128)} %get-tuple-element.174, f32[8,512,512]{2,1,0:T(8,128)} %gather_fusion.2, pred[8]{0:T(512)(128)(4,1)S(1)} %get-tuple-element.162, f32[8,64,512]{2,1,0:T(8,128)S(1)} %gather_fusion.3, f32[8]{0:T(128)S(1)} %gather_fusion.4, ...), kind=kOutput, calls=%fused_computation.17.clone.1 | convolution fusion | flops 1613234176 | bytes 10486320 | tf_op jit(solution)/shard_map/while/body/eval_jaxpr/kij,kjl->kil/dot_general | solution.py:21
  383.5 7.7 gather_fusion.2
  391.2 5.2 gather_fusion.3
  397.0 9.0 %fusion.55 = f32[12,8,64,512]{3,2,1,0:T(8,128)} fusion(f32[12,8,64,512]{3,2,1,0:T(8,128)} %get-tuple-element.175, s32[]{:T(128)} %get-tuple-element.174, f32[8,512,512]{2,1,0:T(8,128)} %gather_fusion.2, pred[8]{0:T(512)(128)(4,1)S(1)} %get-tuple-element.162, f32[8,64,512]{2,1,0:T(8,128)S(1)} %gather_fusion.3, f32[8]{0:T(128)S(1)} %gather_fusion.4, ...), kind=kOutput, calls=%fused_computation.17.clone.1 | convolution fusion | flops 1613234176 | bytes 10486320 | tf_op jit(solution)/shard_map/while/body/eval_jaxpr/kij,kjl->kil/dot_general | solution.py:21
  407.4 7.7 gather_fusion.2
  415.0 5.2 gather_fusion.3
  420.9 9.0 %fusion.55 = f32[12,8,64,512]{3,2,1,0:T(8,128)} fusion(f32[12,8,64,512]{3,2,1,0:T(8,128)} %get-tuple-element.175, s32[]{:T(128)} %get-tuple-element.174, f32[8,512,512]{2,1,0:T(8,128)} %gather_fusion.2, pred[8]{0:T(512)(128)(4,1)S(1)} %get-tuple-element.162, f32[8,64,512]{2,1,0:T(8,128)S(1)} %gather_fusion.3, f32[8]{0:T(128)S(1)} %gather_fusion.4, ...), kind=kOutput, calls=%fused_computation.17.clone.1 | convolution fusion | flops 1613234176 | bytes 10486320 | tf_op jit(solution)/shard_map/while/body/eval_jaxpr/kij,kjl->kil/dot_general | solution.py:21
  431.2 7.7 gather_fusion.2
  438.9 5.2 gather_fusion.3
  444.7 9.0 %fusion.55 = f32[12,8,64,512]{3,2,1,0:T(8,128)} fusion(f32[12,8,64,512]{3,2,1,0:T(8,128)} %get-tuple-element.175, s32[]{:T(128)} %get-tuple-element.174, f32[8,512,512]{2,1,0:T(8,128)} %gather_fusion.2, pred[8]{0:T(512)(128)(4,1)S(1)} %get-tuple-element.162, f32[8,64,512]{2,1,0:T(8,128)S(1)} %gather_fusion.3, f32[8]{0:T(128)S(1)} %gather_fusion.4, ...), kind=kOutput, calls=%fused_computation.17.clone.1 | convolution fusion | flops 1613234176 | bytes 10486320 | tf_op jit(solution)/shard_map/while/body/eval_jaxpr/kij,kjl->kil/dot_general | solution.py:21
  455.0 7.7 gather_fusion.2
  462.7 5.2 gather_fusion.3
  468.6 9.0 %fusion.55 = f32[12,8,64,512]{3,2,1,0:T(8,128)} fusion(f32[12,8,64,512]{3,2,1,0:T(8,128)} %get-tuple-element.175, s32[]{:T(128)} %get-tuple-element.174, f32[8,512,512]{2,1,0:T(8,128)} %gather_fusion.2, pred[8]{0:T(512)(128)(4,1)S(1)} %get-tuple-element.162, f32[8,64,512]{2,1,0:T(8,128)S(1)} %gather_fusion.3, f32[8]{0:T(128)S(1)} %gather_fusion.4, ...), kind=kOutput, calls=%fused_computation.17.clone.1 | convolution fusion | flops 1613234176 | bytes 10486320 | tf_op jit(solution)/shard_map/while/body/eval_jaxpr/kij,kjl->kil/dot_general | solution.py:21
  478.9 7.7 gather_fusion.2
  486.5 5.2 gather_fusion.3
  492.4 9.0 %fusion.55 = f32[12,8,64,512]{3,2,1,0:T(8,128)} fusion(f32[12,8,64,512]{3,2,1,0:T(8,128)} %get-tuple-element.175, s32[]{:T(128)} %get-tuple-element.174, f32[8,512,512]{2,1,0:T(8,128)} %gather_fusion.2, pred[8]{0:T(512)(128)(4,1)S(1)} %get-tuple-element.162, f32[8,64,512]{2,1,0:T(8,128)S(1)} %gather_fusion.3, f32[8]{0:T(128)S(1)} %gather_fusion.4, ...), kind=kOutput, calls=%fused_computation.17.clone.1 | convolution fusion | flops 1613234176 | bytes 10486320 | tf_op jit(solution)/shard_map/while/body/eval_jaxpr/kij,kjl->kil/dot_general | solution.py:21
  502.7 7.7 gather_fusion.2
  510.4 5.2 gather_fusion.3
  516.2 9.0 %fusion.55 = f32[12,8,64,512]{3,2,1,0:T(8,128)} fusion(f32[12,8,64,512]{3,2,1,0:T(8,128)} %get-tuple-element.175, s32[]{:T(128)} %get-tuple-element.174, f32[8,512,512]{2,1,0:T(8,128)} %gather_fusion.2, pred[8]{0:T(512)(128)(4,1)S(1)} %get-tuple-element.162, f32[8,64,512]{2,1,0:T(8,128)S(1)} %gather_fusion.3, f32[8]{0:T(128)S(1)} %gather_fusion.4, ...), kind=kOutput, calls=%fused_computation.17.clone.1 | convolution fusion | flops 1613234176 | bytes 10486320 | tf_op jit(solution)/shard_map/while/body/eval_jaxpr/kij,kjl->kil/dot_general | solution.py:21
  526.6 7.7 gather_fusion.2
  534.2 5.2 gather_fusion.3
  540.1 9.0 %fusion.55 = f32[12,8,64,512]{3,2,1,0:T(8,128)} fusion(f32[12,8,64,512]{3,2,1,0:T(8,128)} %get-tuple-element.175, s32[]{:T(128)} %get-tuple-element.174, f32[8,512,512]{2,1,0:T(8,128)} %gather_fusion.2, pred[8]{0:T(512)(128)(4,1)S(1)} %get-tuple-element.162, f32[8,64,512]{2,1,0:T(8,128)S(1)} %gather_fusion.3, f32[8]{0:T(128)S(1)} %gather_fusion.4, ...), kind=kOutput, calls=%fused_computation.17.clone.1 | convolution fusion | flops 1613234176 | bytes 10486320 | tf_op jit(solution)/shard_map/while/body/eval_jaxpr/kij,kjl->kil/dot_general | solution.py:21
  549.1 6.2 broadcast_in_dim.95
  555.2 23.1 %scatter_fusion = f32[96,64,512]{2,1,0:T(8,128)} fusion(f32[96,64,512]{2,1,0:T(8,128)} %broadcast_in_dim.95, s32[96]{0:T(128)S(1)} %fusion.36, f32[96,64,512]{2,1,0:T(8,128)} %bitcast.217), kind=kCustom, calls=%fused_computation.10 | custom fusion | bytes 37749120 | tf_op jit(solution)/shard_map/scatter | solution.py:89
  578.3 7.9 all-to-all-start.4
  586.4 179.0 %all-to-all-done.4 = f32[16,6,64,512]{3,2,1,0:T(8,128)} async-done(((f32[16,6,64,512]{3,2,1,0:T(8,128)}), f32[16,6,64,512]{3,2,1,0:T(8,128)}, u32[]{:S(2)}, u32[]{:S(2)}) %all-to-all-start.4) | async-done | bytes 12582944 | tf_op jit(solution)/shard_map/all_to_all | solution.py:97
  765.4 15.2 %fusion.20 = f32[1,64,512]{2,0,1:T(1,128)S(1)} fusion(pred[96,1,1]{0,1,2:T(4,128)(4,1)S(1)} %reshape.691, f32[12,8,64,512]{3,2,1,0:T(8,128)} %bitcast.78), kind=kOutput, calls=%fused_computation.35 | convolution fusion | flops 37748736 | bytes 12714080 | tf_op jit(solution)/shard_map/nr,nx->rx/dot_general | solution.py:115
  780.7 0.7 fusion.23
  (154 shorter events, 25.6 us)
Async XLA Ops:
  6.5 43.9 %copy-start = (s32[32]{0:T(128)S(1)}, s32[32]{0:T(128)}, u32[]{:S(2)}) copy-start(s32[32]{0:T(128)} %param.24) | copy-start | bytes 388
  6.5 256.4 %all-gather.2.cloned.1.call-start = ((), (), s32[]{:S(2)}) async-start(), calls=%async_computation.5 | async-start | bytes 9437184 | tf_op jit(solution)/shard_map/all_gather | solution.py:52
  52.3 15.8 %all-to-all-start.3 = ((s32[16,1,6]{2,1,0:T(1,128)}), s32[16,1,6]{2,1,0:T(1,128)S(1)}, u32[]{:S(2)}, u32[]{:S(2)}) async-start(s32[16,1,6]{2,1,0:T(1,128)} %bitcast.55), calls=%async_computation.3 | async-start | bytes 16384 | tf_op jit(solution)/shard_map/all_to_all | solution.py:72
  68.1 7.4 copy-start.6
  68.1 9.0 %copy-start.4 = (s32[8]{0:T(128)S(1)}, s32[8]{0:T(128)}, u32[]{:S(2)}) copy-start(s32[8]{0:T(128)} %param.25) | copy-start | bytes 100
  68.1 12.1 %copy-start.2 = (s32[1,96]{1,0:T(1,128)S(1)}, s32[1,96]{1,0:T(1,128)}, u32[]{:S(2)}) copy-start(s32[1,96]{1,0:T(1,128)} %param.20) | copy-start | bytes 1156
  68.1 188.7 %all-to-all-start.2 = ((f32[16,6,64,512]{3,2,1,0:T(8,128)}), f32[16,6,64,512]{3,2,1,0:T(8,128)}, u32[]{:S(2)}, u32[]{:S(2)}) async-start(f32[16,6,64,512]{3,2,1,0:T(8,128)} %broadcast_select_fusion), calls=%async_computation.2 | async-start | bytes 25165824 | tf_op jit(solution)/shard_map/all_to_all | solution.py:71
  256.8 321.5 %all-to-all-start = ((s32[16,1,6]{2,1,0:T(1,128)}), s32[16,1,6]{2,1,0:T(1,128)S(1)}, u32[]{:S(2)}, u32[]{:S(2)}) async-start(s32[16,1,6]{2,1,0:T(1,128)} %bitcast.40), calls=%async_computation | async-start | bytes 16384 | tf_op jit(solution)/shard_map/all_to_all | solution.py:104
  578.3 187.1 %all-to-all-start.4 = ((f32[16,6,64,512]{3,2,1,0:T(8,128)}), f32[16,6,64,512]{3,2,1,0:T(8,128)}, u32[]{:S(2)}, u32[]{:S(2)}) async-start(f32[16,6,64,512]{3,2,1,0:T(8,128)} %bitcast.215), calls=%async_computation.4 | async-start | bytes 25165824 | tf_op jit(solution)/shard_map/all_to_all | solution.py:97
  586.2 194.4 %copy-start.3 = (f32[1,64,512]{2,1,0:T(8,128)S(1)}, f32[1,64,512]{2,1,0:T(8,128)}, u32[]{:S(2)}) copy-start(f32[1,64,512]{2,1,0:T(8,128)} %param.16) | copy-start | bytes 393220
  586.2 194.4 %copy-start.5 = (f32[512]{0:T(512)S(1)}, f32[512]{0:T(512)}, u32[]{:S(2)}) copy-start(f32[512]{0:T(512)} %param.18) | copy-start | bytes 6148
  586.2 194.4 %copy-start.7 = (f32[1,64]{1,0:T(1,128)S(1)}, f32[1,64]{1,0:T(1,128)}, u32[]{:S(2)}) copy-start(f32[1,64]{1,0:T(1,128)} %param.17) | copy-start | bytes 772
  586.3 195.1 %copy-start.1 = (s32[32]{0:T(128)S(1)}, s32[32]{0:T(128)}, u32[]{:S(2)}) copy-start(s32[32]{0:T(128)} %param.24) | copy-start | bytes 388
Sparse Core Ops, SparseCore 0:
  9.0 52.0 all-gather.1
where the time goes:
time: 790 us; the launch traced here: 788 us
  waiting for transfers between devices  351 us (44%)
  local copies, waits for them, and re-layouts  225 us (28%)
  matrix products  123 us (16%)
  other arithmetic  33.5 us (4%)
  starting transfers between devices  24.8 us (3%)
  blocking collectives  15.5 us (2%)
  between operations  14.3 us (2%)
    all_to_all x1, waiting for transfers between devices, on_device(): lax.all_to_all(outgoing.reshape(lane_count, bucket, tile_rows, window), '...  179 us
    all_to_all x1, waiting for transfers between devices, on_device(): lax.all_to_all(asked_tiles, 'wide', split_axis=0, concat_axis=0, tiled=True)  172 us
    dot_general x12, matrix products, block_product(): jnp.einsum('kij,kjl->kil', tiles_here, weights_here, precision=lax.Precis...  108 us
    gather x24, local copies, waits for them, and re-layouts, block_product(): weights_here = jnp.take(all_integrals, int_ids[task_block], axis=0)  99.8 us
    gather x24, local copies, waits for them, and re-layouts, block_product(): tiles_here = jnp.take(tile_source, tile_index[task_block], axis=0)  69.9 us
    scatter x1, local copies, waits for them, and re-layouts, on_device(): outgoing = jnp.zeros((lane_count * bucket, tile_rows, window), jnp.float3...  23.1 us
  transfers between devices with their start and end apart: 5, of which 2 were waited for; matrix products, arithmetic and copies ran while one was open for 46% of the time, Pallas kernels for 0%

commit v1 on v0

v1 whole, which is shorter than its diff:
```python
import jax
import jax.numpy as jnp
from jax import lax
from jax.experimental import pallas as pl
from jax.experimental.pallas import tpu as pltpu
from jax.sharding import PartitionSpec as P

MESH = pl.DeviceIdType.MESH
f32, bf16, i32 = jnp.float32, jnp.bfloat16, jnp.int32


def iota(shape, dim):
    return lax.broadcasted_iota(i32, shape, dim)


def split(v):
    hi = v.astype(bf16)
    return hi, (v - hi.astype(f32)).astype(bf16)


def mm(a, b):
    return jnp.dot(a, b, preferred_element_type=f32)


def kernel(
    amp,
    integ,
    base,
    pack,
    out,
    a_buf,
    ib,
    shi,
    slo,
    tk,
    acc,
    tb,
    rbuf,
    a_sem,
    own_sem,
    t_send,
    t_recv,
    x_send,
    x_recv,
    q_send,
    q_recv,
    c_send,
    c_recv,
    r_send,
    r_recv,
):
    g = lax.axis_index("grp")
    w = lax.axis_index("wide")
    x, s = g // 2, g % 2
    z, y = w // 4, w % 4
    par = (y + z) % 2
    right = {"grp": ((x + 1) % 4) * 2 + s, "wide": w}
    left = {"grp": ((x + 3) % 4) * 2 + s, "wide": w}
    twin = {"grp": x * 2 + 1 - s, "wide": w}
    sides = (
        {"grp": g, "wide": z * 4 + (y + 1) % 4},
        {"grp": g, "wide": z * 4 + (y + 3) % 4},
        {"grp": g, "wide": ((z + 1) % 4) * 4 + y},
        {"grp": g, "wide": ((z + 3) % 4) * 4 + y},
    )
    mine = par * 256
    theirs = (1 - par) * 256
    own = g

    def remote(src, dst, send, recv, dev):
        return pltpu.make_async_remote_copy(
            src_ref=src,
            dst_ref=dst,
            send_sem=send,
            recv_sem=recv,
            device_id=dev,
            device_id_type=MESH,
        )

    load = pltpu.make_async_copy(amp, a_buf, a_sem)
    load.start()
    loads = []
    for h in range(2):
        loads.append(
            pltpu.make_async_copy(
                integ.at[0, :, pl.ds(h * 256, 256)], ib.at[h, own], own_sem.at[h]
            )
        )
        loads[h].start()

    barrier = pltpu.get_barrier_semaphore()
    for dev in (right, left, twin):
        pl.semaphore_signal(barrier, inc=1, device_id=dev, device_id_type=MESH)

    def greet(d, _):
        pl.semaphore_signal(
            barrier, inc=1, device_id={"grp": g, "wide": (w + d) % 16}, device_id_type=MESH
        )
        return 0

    lax.fori_loop(1, 16, greet, 0)
    pl.semaphore_wait(barrier, 18)

    def task_copy(d):
        return remote(
            pack, tb.at[w], t_send.at[d], t_recv.at[d], {"grp": g, "wide": (w + d) % 16}
        )

    lax.fori_loop(1, 16, lambda d, _: (task_copy(d).start(), 0)[1], 0)

    hop = ((3, 0), (1, 1), (3, 1), (1, 0), (2, 0), (2, 1))

    def block(k, flip=0):
        return 2 * ((x + hop[k][0]) % 4) + (1 - s if flip else s)

    def rows(k, lo=0, n=128):
        return pl.ds(mine + hop[k][1] * 128 + lo, n)

    def x_own(h, k):
        r = rows(k)
        return remote(
            integ.at[0, r, pl.ds(h * 256, 256)],
            ib.at[h, own, r],
            x_send.at[h, k],
            x_recv.at[h, k],
            right if k in (0, 2) else left,
        )

    def x_relay(h, k):
        part = ib.at[h, block(k), rows(k)]
        return remote(
            part, part, x_send.at[h, k + 4], x_recv.at[h, k + 4], right if k == 0 else left
        )

    def x_in(h, k):
        part = ib.at[h, block(k), rows(k)]
        return remote(part, part, x_send.at[h, k], x_recv.at[h, k], right)

    def side_out(h, k, e):
        part = ib.at[h, block(k), rows(k, e * 64, 64)]
        return remote(
            part, part, q_send.at[h, k, e], q_recv.at[h, k, e], sides[hop[k][1] * 2 + e]
        )

    def side_in(h, k, e):
        part = ib.at[h, block(k), pl.ds(theirs + hop[k][1] * 128 + e * 64, 64)]
        return remote(part, part, q_send.at[h, k, e], q_recv.at[h, k, e], right)

    def twin_x(h, k, flip=0):
        part = ib.at[h, block(k, flip), rows(k)]
        return remote(part, part, c_send.at[h, 1 + k], c_recv.at[h, 1 + k], twin)

    first = (0, 1, 4)
    second = (2, 3, 5)

    def twin_q(h, j, flip=0):
        part = ib.at[h, block(first[j], flip), pl.ds(theirs, 256)]
        return remote(part, part, c_send.at[h, 7 + j], c_recv.at[h, 7 + j], twin)

    def twin_own(h):
        return remote(
            integ.at[0, :, pl.ds(h * 256, 256)],
            ib.at[h, own],
            c_send.at[h, 0],
            c_recv.at[h, 0],
            twin,
        )

    def twin_own_in(h):
        part = ib.at[h, 2 * x + 1 - s]
        return remote(part, part, c_send.at[h, 0], c_recv.at[h, 0], twin)

    def got_x(h, k):
        x_in(h, k).wait_recv()
        if k < 2:
            x_relay(h, k).start()
        side_out(h, k, 0).start()
        side_out(h, k, 1).start()
        twin_x(h, k).start()

    def got_q(h, j):
        for k in (first[j], second[j]):
            for e in range(2):
                side_in(h, k, e).wait_recv()
        twin_q(h, j).start()

    def got_twin(h, j):
        twin_x(h, first[j], 1).wait_recv()
        twin_x(h, second[j], 1).wait_recv()
        twin_q(h, j, 1).wait_recv()

    for k in (0, 1, 2, 3):
        x_own(0, k).start()
    twin_own(0).start()

    lane, row = iota((128, 128), 1), iota((128, 128), 0)

    def column(values, which):
        return jnp.sum(jnp.where(lane == which, values, 0.0), axis=1, keepdims=True)

    owner = column(pack[3:4, :].astype(f32), row % 16).astype(i32)
    sign_c = column((1 - 2 * (pack[5:6, :] & 1)).astype(f32), row // 16)
    sign_b = (1 - 2 * (pack[4:5, :] & 1)).astype(f32)[:, :32]
    which_c = row // 16
    local = iota((32, 128), 0) + w * 32

    def task_in(d):
        return remote(
            pack,
            tb.at[(w - d + 16) % 16],
            t_send.at[d],
            t_recv.at[d],
            {"grp": g, "wide": (w + d) % 16},
        )

    lax.fori_loop(1, 16, lambda d, _: (task_in(d).wait_recv(), 0)[1], 0)
    tb[w] = pack[...]
    hits, picks = [], []
    for v in range(16):
        names = tb[v]
        hits.append(
            jnp.where(
                (names[1:2, :] == which_c) & (names[2:3, :] == owner), 1.0, 0.0
            ).astype(bf16)
        )
        picks.append(jnp.where(names[0:1, :] == local, 1.0, 0.0).astype(bf16))
    t = lax.dot_general(
        jnp.concatenate(hits, axis=1),
        jnp.concatenate(picks, axis=1),
        (((1,), (1,)), ((), ())),
        preferred_element_type=f32,
    )
    t = (t * sign_b * sign_c).astype(bf16)
    spread = jnp.where(iota((32, 256), 0) == iota((32, 256), 1) // 8, 1.0, 0.0).astype(bf16)
    lift = jnp.where(iota((1024, 128), 1) == iota((1024, 128), 0) // 8, 1.0, 0.0).astype(bf16)
    wide_t = mm(lift, mm(t, spread).astype(bf16))
    tk[...] = jnp.where(
        iota((1024, 256), 0) % 8 == iota((1024, 256), 1) % 8, wide_t, 0.0
    ).astype(bf16)

    load.wait()

    def form(i, _):
        @pl.when(i == 1)
        def _():
            got_x(0, 0)
            got_x(0, 1)
            for k in (0, 1, 2, 3):
                x_own(1, k).start()
            twin_own(1).start()

        @pl.when(i == 4)
        def _():
            got_x(0, 2)
            got_x(0, 3)

        part = a_buf[:, pl.ds(pl.multiple_of(i * 8, 8), 8), :].reshape(256, 512)
        hi, lo = split(part)
        both = mm(tk[...], hi) + mm(tk[...], lo)
        hi, lo = split(both)
        shi[:, i] = hi.reshape(8, 128, 512)
        slo[:, i] = lo.reshape(8, 128, 512)
        return 0

    lax.fori_loop(0, 8, form, 0)

    def rs_copy(h, d):
        p = (w + d) % 16
        return remote(
            acc.at[h, :, p],
            rbuf.at[h, d],
            r_send.at[h, d],
            r_recv.at[h, d],
            {"grp": g, "wide": p},
        )

    def rs_start(h):
        lax.fori_loop(1, 16, lambda d, _: (rs_copy(h, d).start(), 0)[1], 0)

    def before(u, fn):
        pl.when(u == fn[0])(fn[1])

    def events(u):
        @pl.when(u == 0)
        def _():
            got_q(0, 0)
            got_q(0, 1)
            loads[0].wait()
            got_x(0, 4)
            got_x(0, 5)

        @pl.when(u == 1)
        def _():
            twin_own_in(0).wait_recv()

        @pl.when(u == 3)
        def _():
            got_twin(0, 0)

        @pl.when(u == 4)
        def _():
            got_q(0, 2)
            got_x(1, 0)
            got_x(1, 1)

        @pl.when(u == 5)
        def _():
            got_twin(0, 1)

        @pl.when(u == 7)
        def _():
            got_twin(0, 2)
            got_x(1, 2)
            got_x(1, 3)

        @pl.when(u == 8)
        def _():
            rs_start(0)
            loads[1].wait()

        @pl.when(u == 9)
        def _():
            twin_own_in(1).wait_recv()

        @pl.when(u == 10)
        def _():
            got_q(1, 0)
            got_q(1, 1)
            got_x(1, 4)
            got_x(1, 5)

        @pl.when(u == 11)
        def _():
            got_twin(1, 0)

        @pl.when(u == 13)
        def _():
            got_twin(1, 1)

        @pl.when(u == 14)
        def _():
            got_q(1, 2)

        @pl.when(u == 15)
        def _():
            got_twin(1, 2)

    acc[...] = jnp.zeros_like(acc)

    def unit(u, _):
        events(u)
        h, v = u // 8, u % 8
        d = v // 2
        far = (4 - (d + d // 2 - 2 * (d // 3))) % 4
        c = 2 * ((x + far) % 4) + (s + v) % 2
        ihi, ilo = split(ib[h, c])
        sh = shi[c].reshape(1024, 512)
        sl = slo[c].reshape(1024, 512)
        prod = mm(sh, ihi) + mm(sh, ilo) + mm(sl, ihi)
        acc[h] = acc[h] + prod.reshape(8, 16, 8, 256)
        return 0

    lax.fori_loop(0, 16, unit, 0)
    rs_start(1)

    for h in range(2):
        lax.fori_loop(1, 16, lambda d, _: (rs_copy(h, d).wait_recv(), 0)[1], 0)
        cols = pl.ds(h * 256, 256)
        out[:, :, cols] = base[:, :, cols] + acc[h, :, w]

        def add(d, _):
            out[:, :, cols] = out[:, :, cols] + rbuf[h, d]
            return 0

        lax.fori_loop(1, 16, add, 0)

    lax.fori_loop(1, 16, lambda d, _: (task_copy(d).wait_send(), 0)[1], 0)
    for h in range(2):
        for k in range(4):
            x_own(h, k).wait_send()
        for k in range(2):
            x_relay(h, k).wait_send()
        for k in range(6):
            side_out(h, k, 0).wait_send()
            side_out(h, k, 1).wait_send()
            twin_x(h, k).wait_send()
        for j in range(3):
            twin_q(h, j).wait_send()
        twin_own(h).wait_send()
        lax.fori_loop(1, 16, lambda d, _: (rs_copy(h, d).wait_send(), 0)[1], 0)


def fused(amplitudes, integrals, base, pack):
    vmem = pl.BlockSpec(memory_space=pltpu.VMEM)
    hbm = pl.BlockSpec(memory_space=pl.ANY)
    dma = pltpu.SemaphoreType.DMA
    return pl.pallas_call(
        kernel,
        out_shape=jax.ShapeDtypeStruct((8, 8, 512), f32),
        in_specs=[hbm, hbm, vmem, vmem],
        out_specs=vmem,
        scratch_shapes=[
            pltpu.VMEM((32, 64, 512), f32),
            pltpu.VMEM((2, 8, 512, 256), f32),
            pltpu.VMEM((8, 8, 128, 512), bf16),
            pltpu.VMEM((8, 8, 128, 512), bf16),
            pltpu.VMEM((1024, 256), bf16),
            pltpu.VMEM((2, 8, 16, 8, 256), f32),
            pltpu.VMEM((16, 8, 128), i32),
            pltpu.VMEM((2, 16, 8, 8, 256), f32),
            dma,
            dma((2,)),
            dma((16,)),
            dma((16,)),
            dma((2, 6)),
            dma((2, 6)),
            dma((2, 6, 2)),
            dma((2, 6, 2)),
            dma((2, 10)),
            dma((2, 10)),
            dma((2, 16)),
            dma((2, 16)),
        ],
        compiler_params=pltpu.CompilerParams(
            collective_id=0, has_side_effects=True, vmem_limit_bytes=60 * 2**20
        ),
    )(amplitudes, integrals, base, pack)


def line(values):
    return jnp.pad(values, (0, 128 - values.shape[0]))[None]


def on_device(
    amplitudes,
    integrals,
    base_residual,
    occ_gap,
    virt_sum,
    task_amp,
    task_int,
    task_res,
    task_count,
    res_owner,
    amp_label,
    int_label,
):
    slot = jnp.arange(128, dtype=i32)[None]
    amp = jnp.where(slot < task_count[0], line(task_amp[0]), -1)
    pack = jnp.concatenate(
        [
            amp,
            line(task_int[0]),
            line(task_res[0]),
            line(res_owner[0]),
            line(amp_label),
            line(int_label),
            jnp.zeros((2, 128), i32),
        ],
        axis=0,
    )
    summed = fused(amplitudes, integrals, base_residual.reshape(8, 8, 512), pack)
    divisor = occ_gap[:, :, None] + virt_sum[None, None, :]
    return summed.reshape(1, 64, 512) / divisor


def solution(mesh):
    both = ("grp", "wide")
    return jax.shard_map(
        on_device,
        mesh=mesh,
        in_specs=(
            P(both, None, None),
            P("grp", None, None),
            P(both, None, None),
            P(both, None),
            P(),
            P(both, None),
            P(both, None),
            P(both, None),
            P(both),
            P("grp", None),
            P(both),
            P(),
        ),
        out_specs=P(both, None, None),
        check_vma=False,
    )
```

time: 790 us -> 72.9 us (0.09)
  waiting for transfers between devices: 351 us -> 0 us
  local copies, waits for them, and re-layouts: 225 us -> 1.97 us
  matrix products: 123 us -> 0 us
  Pallas kernels: 0 us -> 67 us
  other arithmetic: 33.5 us -> 2.33 us
  starting transfers between devices: 24.8 us -> 0 us
  blocking collectives: 15.5 us -> 0 us
  between operations: 14.3 us -> 0.71 us
    all_to_all x4 -> x0, waiting for transfers between devices: 351 us -> none  [the longest x1 179 us: on_device(): lax.all_to_all(outgoing.reshape(lane_count, bucket, tile_rows, window), '...]
    gather x66 -> x0, local copies, waits for them, and re-layouts: 192 us -> none  [the longest x24 99.8 us: block_product(): weights_here = jnp.take(all_integrals, int_ids[task_block], axis=0)]
    dot_general x13 -> x0, matrix products: 123 us -> none  [the longest x12 108 us: block_product(): jnp.einsum('kij,kjl->kil', tiles_here, weights_here, precision=lax.Precis...]
    pallas_call x0 -> x1, Pallas kernels: none -> 67 us  [fused(): pl.pallas_call(kernel, out_shape=jax.ShapeDtypeStruct((8, 8, 512), f32),...]
    select_n x32 -> x1, other arithmetic: 29.3 us -> 0.68 us  [on_device(): amp = jnp.where(slot < task_count[0], line(task_amp[0]), -1)]
    scatter x3 -> x0, local copies, waits for them, and re-layouts: 24.8 us -> none  [the longest x1 23.1 us: on_device(): outgoing = jnp.zeros((lane_count * bucket, tile_rows, window), jnp.float3...]
    all_to_all x4 -> x0, starting transfers between devices: 24.8 us -> none  [the longest x1 7.87 us: on_device(): lax.all_to_all(outgoing.reshape(lane_count, bucket, tile_rows, window), '...]
    all_to_all x1 -> x0, blocking collectives: 15.5 us -> none  [on_device(): lax.all_to_all(requests.reshape(lane_count, bucket), 'wide', split_axis=0...]
  transfers between devices with their start and end apart: 5 -> 0, of which waited for: 2 -> 0; matrix products, arithmetic and copies ran while one was open for 46% -> 0% of each run, Pallas kernels for 0% -> 0%
where the time goes in v1:
time: 72.9 us; the launch traced here: 72 us
  Pallas kernels  67 us (92%)
  other arithmetic  2.33 us (3%)
  local copies, waits for them, and re-layouts  1.97 us (3%)
    pallas_call x1, Pallas kernels, fused(): pl.pallas_call(kernel, out_shape=jax.ShapeDtypeStruct((8, 8, 512), f32),...  67 us
    div x1, other arithmetic, on_device(): return summed.reshape(1, 64, 512) / divisor  1.65 us

profile of v1, /device:TPU:0, one launch (start us, length us, event | category | flops | bytes accessed | tf_op | source)
XLA Modules:
  0.0 72.0 jit_solution(12162587638420262415)
XLA Ops:
  0.0 0.0 copy-start
  0.0 0.0 copy-start.1
  0.7 0.7 fusion
  1.4 0.7 pad_bitcast_fusion.3
  2.0 0.7 pad_bitcast_fusion.1
  2.7 0.6 concatenate.3.pack
  3.3 67.0 %shard_map.121 = f32[8,8,512]{2,1,0:T(8,128)} custom-call(f32[32,64,512]{2,1,0:T(8,128)} %amp.1, f32[1,512,512]{2,1,0:T(8,128)} %integ.1, f32[8,8,512]{2,1,0:T(8,128)} %bitcast.22, s32[8,128]{1,0:T(8,128)} %concatenate.3.pack), custom_call_target="tpu_custom_call" | custom-call | tf_op jit(solution)/shard_map/pallas_call | solution.py:397
  70.3 0.0 copy-done
  70.3 0.0 copy-done.1
  70.3 1.7 %bitcast_divide_fusion = f32[1,64,512]{2,1,0:T(8,128)} fusion(f32[8,8,512]{2,1,0:T(8,128)} %shard_map.121, f32[512]{0:T(512)S(1)} %copy-done, f32[64]{0:T(128)S(1)} %bitcast.23), kind=kLoop, calls=%fused_computation | loop fusion | flops 65536 | bytes 264448 | tf_op jit(solution)/shard_map/div | solution.py:464
  (1 shorter events, 0.0 us)
Async XLA Ops:
  0.0 70.3 %copy-start = (f32[512]{0:T(512)S(1)}, f32[512]{0:T(512)}, u32[]{:S(2)}) copy-start(f32[512]{0:T(512)} %param.16) | copy-start | bytes 6148
  0.0 70.3 %copy-start.1 = (f32[1,64]{1,0:T(1,128)S(1)}, f32[1,64]{1,0:T(1,128)}, u32[]{:S(2)}) copy-start(f32[1,64]{1,0:T(1,128)} %param.15) | copy-start | bytes 772

commit v2 on v1

--- a/solution.py
+++ b/solution.py
@@ -35,7 +35,9 @@
     tk,
     acc,
     tb,
-    rbuf,
+    far,
+    near,
+    fin,
     a_sem,
     own_sem,
     t_send,
@@ -46,8 +48,12 @@
     q_recv,
     c_send,
     c_recv,
-    r_send,
-    r_recv,
+    f_send,
+    f_recv,
+    n_send,
+    n_recv,
+    e_send,
+    e_recv,
 ):
     g = lax.axis_index("grp")
     w = lax.axis_index("wide")
@@ -66,6 +72,8 @@
     mine = par * 256
     theirs = (1 - par) * 256
     own = g
+    along_z = [{"grp": g, "wide": ((z + d) % 4) * 4 + y} for d in range(4)]
+    along_y = [{"grp": g, "wide": z * 4 + (y + d) % 4} for d in range(4)]
 
     def remote(src, dst, send, recv, dev):
         return pltpu.make_async_remote_copy(
@@ -89,24 +97,23 @@
         loads[h].start()
 
     barrier = pltpu.get_barrier_semaphore()
-    for dev in (right, left, twin):
+    for dev in (right, left, twin, *along_z[1:], *along_y[1:]):
         pl.semaphore_signal(barrier, inc=1, device_id=dev, device_id_type=MESH)
-
-    def greet(d, _):
-        pl.semaphore_signal(
-            barrier, inc=1, device_id={"grp": g, "wide": (w + d) % 16}, device_id_type=MESH
-        )
-        return 0
-
-    lax.fori_loop(1, 16, greet, 0)
-    pl.semaphore_wait(barrier, 18)
-
-    def task_copy(d):
-        return remote(
-            pack, tb.at[w], t_send.at[d], t_recv.at[d], {"grp": g, "wide": (w + d) % 16}
-        )
-
-    lax.fori_loop(1, 16, lambda d, _: (task_copy(d).start(), 0)[1], 0)
+    pl.semaphore_wait(barrier, 9)
+
+    def task_z(d, back=0):
+        return remote(
+            pack, tb.at[y, (z - d if back else z) % 4], t_send.at[d], t_recv.at[d], along_z[d]
+        )
+
+    def task_y(d, back=0):
+        part = tb.at[(y - d if back else y) % 4]
+        return remote(part, part, t_send.at[4 + d], t_recv.at[4 + d], along_y[d])
+
+    for d in (2, 1, 3):
+        task_z(d).start()
+    keep = pltpu.make_async_copy(pack, tb.at[y, z], t_send.at[0])
+    keep.start()
 
     hop = ((3, 0), (1, 1), (3, 1), (1, 0), (2, 0), (2, 1))
 
@@ -203,27 +210,28 @@
     sign_b = (1 - 2 * (pack[4:5, :] & 1)).astype(f32)[:, :32]
     which_c = row // 16
     local = iota((32, 128), 0) + w * 32
-
-    def task_in(d):
-        return remote(
-            pack,
-            tb.at[(w - d + 16) % 16],
-            t_send.at[d],
-            t_recv.at[d],
-            {"grp": g, "wide": (w + d) % 16},
-        )
-
-    lax.fori_loop(1, 16, lambda d, _: (task_in(d).wait_recv(), 0)[1], 0)
-    tb[w] = pack[...]
+    real = iota((32, 128), 1) < 96
+
+    keep.wait()
+    for d in (1, 3, 2):
+        task_z(d, 1).wait_recv()
+    for d in (2, 1, 3):
+        task_y(d).start()
+    got_x(0, 0)
+    got_x(0, 1)
+    for d in (1, 3, 2):
+        task_y(d, 1).wait_recv()
     hits, picks = [], []
     for v in range(16):
-        names = tb[v]
+        names = tb[v // 4, v % 4]
         hits.append(
             jnp.where(
                 (names[1:2, :] == which_c) & (names[2:3, :] == owner), 1.0, 0.0
             ).astype(bf16)
         )
-        picks.append(jnp.where(names[0:1, :] == local, 1.0, 0.0).astype(bf16))
+        picks.append(
+            jnp.where((names[0:1, :] == local) & real, 1.0, 0.0).astype(bf16)
+        )
     t = lax.dot_general(
         jnp.concatenate(hits, axis=1),
         jnp.concatenate(picks, axis=1),
@@ -241,15 +249,13 @@
     load.wait()
 
     def form(i, _):
-        @pl.when(i == 1)
+        @pl.when(i == 0)
         def _():
-            got_x(0, 0)
-            got_x(0, 1)
             for k in (0, 1, 2, 3):
                 x_own(1, k).start()
             twin_own(1).start()
 
-        @pl.when(i == 4)
+        @pl.when(i == 3)
         def _():
             got_x(0, 2)
             got_x(0, 3)
@@ -264,117 +270,150 @@
 
     lax.fori_loop(0, 8, form, 0)
 
-    def rs_copy(h, d):
-        p = (w + d) % 16
-        return remote(
-            acc.at[h, :, p],
-            rbuf.at[h, d],
-            r_send.at[h, d],
-            r_recv.at[h, d],
-            {"grp": g, "wide": p},
-        )
-
-    def rs_start(h):
-        lax.fori_loop(1, 16, lambda d, _: (rs_copy(h, d).start(), 0)[1], 0)
-
-    def before(u, fn):
-        pl.when(u == fn[0])(fn[1])
+    lo, hi = pl.ds(0, 2), pl.ds(2, 2)
+    every = pl.ds(0, 4)
+
+    def part(h, a, f, e):
+        if a == 0:
+            return (h, slice(None), (z + f) % 4, e, slice(None), pl.ds(0, 128))
+        return (h, slice(None), e, (y + f) % 4, slice(None), pl.ds(128, 128))
+
+    def first_axis(a):
+        return along_y if a else along_z
+
+    def second_axis(a):
+        return along_z if a else along_y
+
+    def rs_far(h, a, v):
+        return remote(
+            acc.at[part(h, a, 2, hi if v else lo)],
+            far.at[h, a, v],
+            f_send.at[h, a, v],
+            f_recv.at[h, a, v],
+            first_axis(a)[3 if v else 1],
+        )
+
+    def rs_near(h, a, v, late):
+        e = (lo, hi)[1 - v] if not late else (lo, hi)[v]
+        return remote(
+            acc.at[part(h, a, 3 if v else 1, e)],
+            near.at[h, a, v, :, e],
+            n_send.at[h, a, v, late],
+            n_recv.at[h, a, v, late],
+            first_axis(a)[3 if v else 1],
+        )
+
+    def rs_last(h, a, d):
+        to = (slice(None), ((z if a else y) + d) % 4)
+        return remote(
+            near.at[(h, a, 0) + to],
+            fin.at[h, a, d],
+            e_send.at[h, a, d],
+            e_recv.at[h, a, d],
+            second_axis(a)[d],
+        )
+
+    ways = [(a, v) for v in range(2) for a in range(2)]
+
+    def rs_one(h):
+        for a, v in ways:
+            rs_far(h, a, v).start()
+        for a, v in ways:
+            rs_near(h, a, v, 0).start()
+
+    def rs_two(h):
+        for a, v in ways:
+            rs_far(h, a, v).wait_recv()
+            at = part(h, a, 3 if v else 1, hi if v else lo)
+            acc[at] = acc[at] + far[h, a, v]
+        for a, v in ways:
+            rs_near(h, a, v, 1).start()
+
+    def rs_three(h):
+        for a in range(2):
+            for v in range(2):
+                for late in range(2):
+                    rs_near(h, a, v, late).wait_recv()
+            near[h, a, 0] = near[h, a, 0] + near[h, a, 1] + acc[part(h, a, 0, every)]
+        for d in (2, 1, 3):
+            for a in range(2):
+                rs_last(h, a, d).start()
+
+    def rs_end(h):
+        for a in range(2):
+            for d in (1, 3, 2):
+                rs_last(h, a, d).wait_recv()
+            cols = pl.ds(h * 256 + a * 128, 128)
+            out[:, :, cols] = (
+                base[:, :, cols]
+                + near[h, a, 0, :, z if a else y]
+                + fin[h, a, 1]
+                + fin[h, a, 2]
+                + fin[h, a, 3]
+            )
 
     def events(u):
-        @pl.when(u == 0)
-        def _():
+        if u == 0:
+            got_x(0, 4)
+            got_x(0, 5)
             got_q(0, 0)
             got_q(0, 1)
             loads[0].wait()
-            got_x(0, 4)
-            got_x(0, 5)
-
-        @pl.when(u == 1)
-        def _():
+        if u == 1:
             twin_own_in(0).wait_recv()
-
-        @pl.when(u == 3)
-        def _():
+        if u == 3:
             got_twin(0, 0)
-
-        @pl.when(u == 4)
-        def _():
-            got_q(0, 2)
             got_x(1, 0)
             got_x(1, 1)
-
-        @pl.when(u == 5)
-        def _():
+        if u == 4:
+            got_q(0, 2)
+        if u == 5:
             got_twin(0, 1)
-
-        @pl.when(u == 7)
-        def _():
+        if u == 7:
             got_twin(0, 2)
             got_x(1, 2)
             got_x(1, 3)
-
-        @pl.when(u == 8)
-        def _():
-            rs_start(0)
+        if u == 8:
+            rs_one(0)
             loads[1].wait()
-
-        @pl.when(u == 9)
-        def _():
+        if u == 9:
             twin_own_in(1).wait_recv()
-
-        @pl.when(u == 10)
-        def _():
+        if u == 10:
             got_q(1, 0)
             got_q(1, 1)
+        if u == 11:
+            got_twin(1, 0)
+        if u == 12:
             got_x(1, 4)
             got_x(1, 5)
-
-        @pl.when(u == 11)
-        def _():
-            got_twin(1, 0)
-
-        @pl.when(u == 13)
-        def _():
+        if u == 13:
             got_twin(1, 1)
-
-        @pl.when(u == 14)
-        def _():
+            rs_two(0)
+        if u == 14:
             got_q(1, 2)
-
-        @pl.when(u == 15)
-        def _():
+        if u == 15:
             got_twin(1, 2)
 
-    acc[...] = jnp.zeros_like(acc)
-
-    def unit(u, _):
+    for u in range(16):
         events(u)
         h, v = u // 8, u % 8
-        d = v // 2
-        far = (4 - (d + d // 2 - 2 * (d // 3))) % 4
-        c = 2 * ((x + far) % 4) + (s + v) % 2
+        c = 2 * ((x + (0, 3, 1, 2)[v // 2]) % 4) + (1 - s if v % 2 else s)
         ihi, ilo = split(ib[h, c])
         sh = shi[c].reshape(1024, 512)
         sl = slo[c].reshape(1024, 512)
-        prod = mm(sh, ihi) + mm(sh, ilo) + mm(sl, ihi)
-        acc[h] = acc[h] + prod.reshape(8, 16, 8, 256)
-        return 0
-
-    lax.fori_loop(0, 16, unit, 0)
-    rs_start(1)
-
-    for h in range(2):
-        lax.fori_loop(1, 16, lambda d, _: (rs_copy(h, d).wait_recv(), 0)[1], 0)
-        cols = pl.ds(h * 256, 256)
-        out[:, :, cols] = base[:, :, cols] + acc[h, :, w]
-
-        def add(d, _):
-            out[:, :, cols] = out[:, :, cols] + rbuf[h, d]
-            return 0
-
-        lax.fori_loop(1, 16, add, 0)
-
-    lax.fori_loop(1, 16, lambda d, _: (task_copy(d).wait_send(), 0)[1], 0)
+        prod = (mm(sh, ihi) + mm(sh, ilo) + mm(sl, ihi)).reshape(8, 4, 4, 8, 256)
+        acc[h] = prod if v == 0 else acc[h] + prod
+
+    rs_one(1)
+    rs_three(0)
+    rs_two(1)
+    rs_end(0)
+    rs_three(1)
+    rs_end(1)
+
+    for d in (1, 2, 3):
+        task_z(d).wait_send()
+        task_y(d).wait_send()
     for h in range(2):
         for k in range(4):
             x_own(h, k).wait_send()
@@ -387,7 +426,13 @@
         for j in range(3):
             twin_q(h, j).wait_send()
         twin_own(h).wait_send()
-        lax.fori_loop(1, 16, lambda d, _: (rs_copy(h, d).wait_send(), 0)[1], 0)
+        for a, v in ways:
+            rs_far(h, a, v).wait_send()
+            rs_near(h, a, v, 0).wait_send()
+            rs_near(h, a, v, 1).wait_send()
+        for a in range(2):
+            for d in (1, 2, 3):
+                rs_last(h, a, d).wait_send()
 
 
 def fused(amplitudes, integrals, base, pack):
@@ -405,21 +450,27 @@
             pltpu.VMEM((8, 8, 128, 512), bf16),
             pltpu.VMEM((8, 8, 128, 512), bf16),
             pltpu.VMEM((1024, 256), bf16),
-            pltpu.VMEM((2, 8, 16, 8, 256), f32),
-            pltpu.VMEM((16, 8, 128), i32),
-            pltpu.VMEM((2, 16, 8, 8, 256), f32),
+            pltpu.VMEM((2, 8, 4, 4, 8, 256), f32),
+            pltpu.VMEM((4, 4, 8, 128), i32),
+            pltpu.VMEM((2, 2, 2, 8, 2, 8, 128), f32),
+            pltpu.VMEM((2, 2, 2, 8, 4, 8, 128), f32),
+            pltpu.VMEM((2, 2, 4, 8, 8, 128), f32),
             dma,
             dma((2,)),
-            dma((16,)),
-            dma((16,)),
+            dma((8,)),
+            dma((8,)),
             dma((2, 6)),
             dma((2, 6)),
             dma((2, 6, 2)),
             dma((2, 6, 2)),
             dma((2, 10)),
             dma((2, 10)),
-            dma((2, 16)),
-            dma((2, 16)),
+            dma((2, 2, 2)),
+            dma((2, 2, 2)),
+            dma((2, 2, 2, 2)),
+            dma((2, 2, 2, 2)),
+            dma((2, 2, 4)),
+            dma((2, 2, 4)),
         ],
         compiler_params=pltpu.CompilerParams(
             collective_id=0, has_side_effects=True, vmem_limit_bytes=60 * 2**20
@@ -427,8 +478,9 @@
     )(amplitudes, integrals, base, pack)
 
 
-def line(values):
-    return jnp.pad(values, (0, 128 - values.shape[0]))[None]
+def line(values, row):
+    values = values.reshape(1, -1)
+    return jnp.pad(values, ((row, 7 - row), (0, 128 - values.shape[1])))
 
 
 def on_device(
@@ -445,19 +497,14 @@
     amp_label,
     int_label,
 ):
-    slot = jnp.arange(128, dtype=i32)[None]
-    amp = jnp.where(slot < task_count[0], line(task_amp[0]), -1)
-    pack = jnp.concatenate(
-        [
-            amp,
-            line(task_int[0]),
-            line(task_res[0]),
-            line(res_owner[0]),
-            line(amp_label),
-            line(int_label),
-            jnp.zeros((2, 128), i32),
-        ],
-        axis=0,
+    used = jnp.arange(96, dtype=i32)[None] < task_count[0]
+    pack = (
+        line(jnp.where(used, task_amp, -1), 0)
+        + line(task_int, 1)
+        + line(task_res, 2)
+        + line(res_owner, 3)
+        + line(amp_label, 4)
+        + line(int_label, 5)
     )
     summed = fused(amplitudes, integrals, base_residual.reshape(8, 8, 512), pack)
     divisor = occ_gap[:, :, None] + virt_sum[None, None, :]

time: 72.9 us -> 69 us (0.947)
  Pallas kernels: 67 us -> 64.4 us
  local copies, waits for them, and re-layouts: 1.97 us -> 0.01 us
  other arithmetic: 2.33 us -> 3.64 us
    pallas_call x1, Pallas kernels: 67 us -> 64.4 us  [fused(): pl.pallas_call(kernel, out_shape=jax.ShapeDtypeStruct((8, 8, 512), f32),...]
    broadcast_in_dim x3 -> x0, local copies, waits for them, and re-layouts: 1.35 us -> none  [the longest x2 1.35 us: line(): return jnp.pad(values, (0, 128 - values.shape[0]))[None]]
    add x0 -> x1, other arithmetic: none -> 1.32 us  [on_device(): line(jnp.where(used, task_amp, -1), 0) + line(task_int, 1)]
where the time goes in v2:
time: 69 us; the launch traced here: 68.8 us
  Pallas kernels  64.4 us (93%)
  other arithmetic  3.64 us (5%)
  between operations  0.71 us (1%)
    pallas_call x1, Pallas kernels, fused(): pl.pallas_call(kernel, out_shape=jax.ShapeDtypeStruct((8, 8, 512), f32),...  64.4 us
    div x1, other arithmetic, on_device(): return summed.reshape(1, 64, 512) / divisor  1.65 us

profile of v2, /device:TPU:0, one launch (start us, length us, event | category | flops | bytes accessed | tf_op | source)
XLA Modules:
  0.0 68.8 jit_solution(14910337056367069456)
XLA Ops:
  0.0 0.0 copy-start
  0.0 0.0 copy-start.1
  0.7 0.7 compare_select_fusion
  1.3 1.3 %pad_add_fusion.pack = s32[8,128]{1,0:T(8,128)} fusion(s32[1,8]{1,0:T(1,128)} %bitcast.10, s32[1,32]{1,0:T(1,128)} %bitcast.11, s32[1,16]{1,0:T(1,128)} %param.21, s32[1,96]{1,0:T(1,128)} %param.19, s32[1,96]{1,0:T(1,128)} %param.18, s32[1,96]{1,0:T(1,128)S(1)} %compare_select_fusion), kind=kLoop, calls=%fused_computation.1 | loop fusion | flops 5120 | bytes 5472 | tf_op jit(solution)/shard_map/add | solution.py:502
  2.7 64.4 %shard_map.121 = f32[8,8,512]{2,1,0:T(8,128)} custom-call(f32[32,64,512]{2,1,0:T(8,128)} %amp.1, f32[1,512,512]{2,1,0:T(8,128)} %integ.1, f32[8,8,512]{2,1,0:T(8,128)} %bitcast.8, s32[8,128]{1,0:T(8,128)} %pad_add_fusion.pack), custom_call_target="tpu_custom_call" | custom-call | tf_op jit(solution)/shard_map/pallas_call | solution.py:442
  67.1 0.0 copy-done
  67.1 0.0 copy-done.1
  67.1 1.7 %bitcast_divide_fusion = f32[1,64,512]{2,1,0:T(8,128)} fusion(f32[8,8,512]{2,1,0:T(8,128)} %shard_map.121, f32[512]{0:T(512)S(1)} %copy-done, f32[64]{0:T(128)S(1)} %bitcast.9), kind=kLoop, calls=%fused_computation | loop fusion | flops 65536 | bytes 264448 | tf_op jit(solution)/shard_map/div | solution.py:511
Async XLA Ops:
  0.0 67.1 %copy-start = (f32[512]{0:T(512)S(1)}, f32[512]{0:T(512)}, u32[]{:S(2)}) copy-start(f32[512]{0:T(512)} %param.16) | copy-start | bytes 6148
  0.0 67.1 %copy-start.1 = (f32[1,64]{1,0:T(1,128)S(1)}, f32[1,64]{1,0:T(1,128)}, u32[]{:S(2)}) copy-start(f32[1,64]{1,0:T(1,128)} %param.15) | copy-start | bytes 772

commit v3 on v2

--- a/solution.py
+++ b/solution.py
@@ -399,10 +399,11 @@
         h, v = u // 8, u % 8
         c = 2 * ((x + (0, 3, 1, 2)[v // 2]) % 4) + (1 - s if v % 2 else s)
         ihi, ilo = split(ib[h, c])
-        sh = shi[c].reshape(1024, 512)
-        sl = slo[c].reshape(1024, 512)
-        prod = (mm(sh, ihi) + mm(sh, ilo) + mm(sl, ihi)).reshape(8, 4, 4, 8, 256)
-        acc[h] = prod if v == 0 else acc[h] + prod
+        for r in (slice(0, 4), slice(4, 8)):
+            sh = shi[c, r].reshape(512, 512)
+            sl = slo[c, r].reshape(512, 512)
+            prod = (mm(sh, ihi) + mm(sh, ilo) + mm(sl, ihi)).reshape(4, 4, 4, 8, 256)
+            acc[h, r] = prod if v == 0 else acc[h, r] + prod
 
     rs_one(1)
     rs_three(0)

time: 69 us -> 60.9 us (0.88)
  Pallas kernels: 64.4 us -> 56.4 us
    pallas_call x1, Pallas kernels: 64.4 us -> 56.4 us  [fused(): pl.pallas_call(kernel, out_shape=jax.ShapeDtypeStruct((8, 8, 512), f32),...]
where the time goes in v3:
time: 60.9 us; the launch traced here: 60.7 us
  Pallas kernels  56.4 us (93%)
  other arithmetic  3.64 us (6%)
  between operations  0.71 us (1%)
    pallas_call x1, Pallas kernels, fused(): pl.pallas_call(kernel, out_shape=jax.ShapeDtypeStruct((8, 8, 512), f32),...  56.4 us
    div x1, other arithmetic, on_device(): return summed.reshape(1, 64, 512) / divisor  1.65 us
    add x1, other arithmetic, on_device(): line(jnp.where(used, task_amp, -1), 0) + line(task_int, 1)  1.32 us

profile of v3, /device:TPU:0, one launch (start us, length us, event | category | flops | bytes accessed | tf_op | source)
XLA Modules:
  0.0 60.7 jit_solution(728149306788299432)
XLA Ops:
  0.0 0.0 copy-start
  0.0 0.0 copy-start.1
  0.7 0.7 %compare_select_fusion = s32[1,96]{1,0:T(1,128)S(1)} fusion(s32[1,96]{1,0:T(1,128)} %param.17, s32[]{:T(128)} %bitcast.7), kind=kLoop, calls=%fused_computation.2 | loop fusion | flops 192 | bytes 772 | tf_op jit(solution)/shard_map/jit(_where)/select_n | solution.py:503
  1.3 1.3 %pad_add_fusion.pack = s32[8,128]{1,0:T(8,128)} fusion(s32[1,8]{1,0:T(1,128)} %bitcast.10, s32[1,32]{1,0:T(1,128)} %bitcast.11, s32[1,16]{1,0:T(1,128)} %param.21, s32[1,96]{1,0:T(1,128)} %param.19, s32[1,96]{1,0:T(1,128)} %param.18, s32[1,96]{1,0:T(1,128)S(1)} %compare_select_fusion), kind=kLoop, calls=%fused_computation.1 | loop fusion | flops 5120 | bytes 5472 | tf_op jit(solution)/shard_map/add | solution.py:503
  2.7 56.4 %shard_map.121 = f32[8,8,512]{2,1,0:T(8,128)} custom-call(f32[32,64,512]{2,1,0:T(8,128)} %amp.1, f32[1,512,512]{2,1,0:T(8,128)} %integ.1, f32[8,8,512]{2,1,0:T(8,128)} %bitcast.8, s32[8,128]{1,0:T(8,128)} %pad_add_fusion.pack), custom_call_target="tpu_custom_call" | custom-call | tf_op jit(solution)/shard_map/pallas_call | solution.py:443
  59.0 0.0 copy-done
  59.1 0.0 copy-done.1
  59.1 1.7 %bitcast_divide_fusion = f32[1,64,512]{2,1,0:T(8,128)} fusion(f32[8,8,512]{2,1,0:T(8,128)} %shard_map.121, f32[512]{0:T(512)S(1)} %copy-done, f32[64]{0:T(128)S(1)} %bitcast.9), kind=kLoop, calls=%fused_computation | loop fusion | flops 65536 | bytes 264448 | tf_op jit(solution)/shard_map/div | solution.py:512
Async XLA Ops:
  0.0 59.0 %copy-start = (f32[512]{0:T(512)S(1)}, f32[512]{0:T(512)}, u32[]{:S(2)}) copy-start(f32[512]{0:T(512)} %param.16) | copy-start | bytes 6148
  0.0 59.1 %copy-start.1 = (f32[1,64]{1,0:T(1,128)S(1)}, f32[1,64]{1,0:T(1,128)}, u32[]{:S(2)}) copy-start(f32[1,64]{1,0:T(1,128)} %param.15) | copy-start | bytes 772

commit v4 on v3

--- a/solution.py
+++ b/solution.py
@@ -35,7 +35,6 @@
     tk,
     acc,
     tb,
-    far,
     near,
     fin,
     a_sem,
@@ -48,12 +47,11 @@
     q_recv,
     c_send,
     c_recv,
-    f_send,
-    f_recv,
     n_send,
     n_recv,
     e_send,
     e_recv,
+    ok_sem,
 ):
     g = lax.axis_index("grp")
     w = lax.axis_index("wide")
@@ -101,18 +99,19 @@
         pl.semaphore_signal(barrier, inc=1, device_id=dev, device_id_type=MESH)
     pl.semaphore_wait(barrier, 9)
 
-    def task_z(d, back=0):
-        return remote(
-            pack, tb.at[y, (z - d if back else z) % 4], t_send.at[d], t_recv.at[d], along_z[d]
-        )
-
-    def task_y(d, back=0):
-        part = tb.at[(y - d if back else y) % 4]
-        return remote(part, part, t_send.at[4 + d], t_recv.at[4 + d], along_y[d])
-
-    for d in (2, 1, 3):
-        task_z(d).start()
-    keep = pltpu.make_async_copy(pack, tb.at[y, z], t_send.at[0])
+    for d in range(1, 4):
+        pl.semaphore_signal(ok_sem, inc=1, device_id=along_y[d], device_id_type=MESH)
+
+    def task(dz, dy, back=0):
+        peer = {"grp": g, "wide": ((z + dz) % 4) * 4 + (y + dy) % 4}
+        slot = tb.at[(y - dy) % 4, (z - dz) % 4] if back else tb.at[y, z]
+        return remote(pack, slot, t_send.at[dz, dy], t_recv.at[dz, dy], peer)
+
+    beside = [(dz, 0) for dz in (2, 1, 3)] + [(0, dy) for dy in (2, 1, 3)]
+    beyond = [(dz, dy) for dz in (2, 1, 3) for dy in (2, 1, 3)]
+    for dz, dy in beside:
+        task(dz, dy).start()
+    keep = pltpu.make_async_copy(pack, tb.at[y, z], t_send.at[0, 0])
     keep.start()
 
     hop = ((3, 0), (1, 1), (3, 1), (1, 0), (2, 0), (2, 1))
@@ -196,9 +195,13 @@
         twin_x(h, second[j], 1).wait_recv()
         twin_q(h, j, 1).wait_recv()
 
-    for k in (0, 1, 2, 3):
-        x_own(0, k).start()
-    twin_own(0).start()
+    for h, k in ((0, 0), (0, 1), (0, 2), (0, 3), (1, 0), (1, 1)):
+        x_own(h, k).start()
+    for h in range(2):
+        twin_own(h).start()
+    pl.semaphore_wait(ok_sem, 3)
+    for dz, dy in beyond:
+        task(dz, dy).start()
 
     lane, row = iota((128, 128), 1), iota((128, 128), 0)
 
@@ -213,14 +216,12 @@
     real = iota((32, 128), 1) < 96
 
     keep.wait()
-    for d in (1, 3, 2):
-        task_z(d, 1).wait_recv()
-    for d in (2, 1, 3):
-        task_y(d).start()
     got_x(0, 0)
     got_x(0, 1)
-    for d in (1, 3, 2):
-        task_y(d, 1).wait_recv()
+    for k in (2, 3):
+        x_own(1, k).start()
+    for dz, dy in beside + beyond:
+        task(dz, dy, 1).wait_recv()
     hits, picks = [], []
     for v in range(16):
         names = tb[v // 4, v % 4]
@@ -249,16 +250,22 @@
     load.wait()
 
     def form(i, _):
-        @pl.when(i == 0)
-        def _():
-            for k in (0, 1, 2, 3):
-                x_own(1, k).start()
-            twin_own(1).start()
-
-        @pl.when(i == 3)
+        @pl.when(i == 1)
         def _():
             got_x(0, 2)
             got_x(0, 3)
+
+        @pl.when(i == 4)
+        def _():
+            got_x(1, 0)
+            got_x(1, 1)
+
+        @pl.when(i == 6)
+        def _():
+            got_x(0, 4)
+            got_x(0, 5)
+            got_q(0, 0)
+            got_q(0, 1)
 
         part = a_buf[:, pl.ds(pl.multiple_of(i * 8, 8), 8), :].reshape(256, 512)
         hi, lo = split(part)
@@ -270,7 +277,6 @@
 
     lax.fori_loop(0, 8, form, 0)
 
-    lo, hi = pl.ds(0, 2), pl.ds(2, 2)
     every = pl.ds(0, 4)
 
     def part(h, a, f, e):
@@ -284,23 +290,13 @@
     def second_axis(a):
         return along_z if a else along_y
 
-    def rs_far(h, a, v):
+    def rs_first(h, a, d):
         return remote(
-            acc.at[part(h, a, 2, hi if v else lo)],
-            far.at[h, a, v],
-            f_send.at[h, a, v],
-            f_recv.at[h, a, v],
-            first_axis(a)[3 if v else 1],
-        )
-
-    def rs_near(h, a, v, late):
-        e = (lo, hi)[1 - v] if not late else (lo, hi)[v]
-        return remote(
-            acc.at[part(h, a, 3 if v else 1, e)],
-            near.at[h, a, v, :, e],
-            n_send.at[h, a, v, late],
-            n_recv.at[h, a, v, late],
-            first_axis(a)[3 if v else 1],
+            acc.at[part(h, a, d, every)],
+            near.at[h, a, d],
+            n_send.at[h, a, d],
+            n_recv.at[h, a, d],
+            first_axis(a)[d],
         )
 
     def rs_last(h, a, d):
@@ -313,28 +309,18 @@
             second_axis(a)[d],
         )
 
-    ways = [(a, v) for v in range(2) for a in range(2)]
-
     def rs_one(h):
-        for a, v in ways:
-            rs_far(h, a, v).start()
-        for a, v in ways:
-            rs_near(h, a, v, 0).start()
+        for d in (2, 1, 3):
+            for a in range(2):
+                rs_first(h, a, d).start()
 
     def rs_two(h):
-        for a, v in ways:
-            rs_far(h, a, v).wait_recv()
-            at = part(h, a, 3 if v else 1, hi if v else lo)
-            acc[at] = acc[at] + far[h, a, v]
-        for a, v in ways:
-            rs_near(h, a, v, 1).start()
-
-    def rs_three(h):
         for a in range(2):
-            for v in range(2):
-                for late in range(2):
-                    rs_near(h, a, v, late).wait_recv()
-            near[h, a, 0] = near[h, a, 0] + near[h, a, 1] + acc[part(h, a, 0, every)]
+            for d in (1, 3, 2):
+                rs_first(h, a, d).wait_recv()
+            near[h, a, 0] = (
+                near[h, a, 1] + near[h, a, 2] + near[h, a, 3] + acc[part(h, a, 0, every)]
+            )
         for d in (2, 1, 3):
             for a in range(2):
                 rs_last(h, a, d).start()
@@ -354,43 +340,34 @@
 
     def events(u):
         if u == 0:
-            got_x(0, 4)
-            got_x(0, 5)
-            got_q(0, 0)
-            got_q(0, 1)
             loads[0].wait()
         if u == 1:
             twin_own_in(0).wait_recv()
+            got_x(1, 2)
+            got_x(1, 3)
         if u == 3:
+            got_q(0, 2)
             got_twin(0, 0)
-            got_x(1, 0)
-            got_x(1, 1)
         if u == 4:
-            got_q(0, 2)
+            got_x(1, 4)
+            got_x(1, 5)
         if u == 5:
             got_twin(0, 1)
+        if u == 6:
+            got_q(1, 0)
+            got_q(1, 1)
         if u == 7:
             got_twin(0, 2)
-            got_x(1, 2)
-            got_x(1, 3)
         if u == 8:
             rs_one(0)
             loads[1].wait()
         if u == 9:
             twin_own_in(1).wait_recv()
-        if u == 10:
-            got_q(1, 0)
-            got_q(1, 1)
+            got_q(1, 2)
         if u == 11:
             got_twin(1, 0)
-        if u == 12:
-            got_x(1, 4)
-            got_x(1, 5)
         if u == 13:
             got_twin(1, 1)
-            rs_two(0)
-        if u == 14:
-            got_q(1, 2)
         if u == 15:
             got_twin(1, 2)
 
@@ -406,15 +383,13 @@
             acc[h, r] = prod if v == 0 else acc[h, r] + prod
 
     rs_one(1)
-    rs_three(0)
+    rs_two(0)
     rs_two(1)
     rs_end(0)
-    rs_three(1)
     rs_end(1)
 
-    for d in (1, 2, 3):
-        task_z(d).wait_send()
-        task_y(d).wait_send()
+    for dz, dy in beside + beyond:
+        task(dz, dy).wait_send()
     for h in range(2):
         for k in range(4):
             x_own(h, k).wait_send()
@@ -427,12 +402,9 @@
         for j in range(3):
             twin_q(h, j).wait_send()
         twin_own(h).wait_send()
-        for a, v in ways:
-            rs_far(h, a, v).wait_send()
-            rs_near(h, a, v, 0).wait_send()
-            rs_near(h, a, v, 1).wait_send()
         for a in range(2):
             for d in (1, 2, 3):
+                rs_first(h, a, d).wait_send()
                 rs_last(h, a, d).wait_send()
 
 
@@ -453,25 +425,23 @@
             pltpu.VMEM((1024, 256), bf16),
             pltpu.VMEM((2, 8, 4, 4, 8, 256), f32),
             pltpu.VMEM((4, 4, 8, 128), i32),
-            pltpu.VMEM((2, 2, 2, 8, 2, 8, 128), f32),
-            pltpu.VMEM((2, 2, 2, 8, 4, 8, 128), f32),
+            pltpu.VMEM((2, 2, 4, 8, 4, 8, 128), f32),
             pltpu.VMEM((2, 2, 4, 8, 8, 128), f32),
             dma,
             dma((2,)),
-            dma((8,)),
-            dma((8,)),
+            dma((4, 4)),
+            dma((4, 4)),
             dma((2, 6)),
             dma((2, 6)),
             dma((2, 6, 2)),
             dma((2, 6, 2)),
             dma((2, 10)),
             dma((2, 10)),
-            dma((2, 2, 2)),
-            dma((2, 2, 2)),
-            dma((2, 2, 2, 2)),
-            dma((2, 2, 2, 2)),
             dma((2, 2, 4)),
             dma((2, 2, 4)),
+            dma((2, 2, 4)),
+            dma((2, 2, 4)),
+            pltpu.SemaphoreType.REGULAR,
         ],
         compiler_params=pltpu.CompilerParams(
             collective_id=0, has_side_effects=True, vmem_limit_bytes=60 * 2**20

time: 60.9 us -> 56.9 us (0.934)
  Pallas kernels: 56.4 us -> 52.4 us
    pallas_call x1, Pallas kernels: 56.4 us -> 52.4 us  [fused(): pl.pallas_call(kernel, out_shape=jax.ShapeDtypeStruct((8, 8, 512), f32),...]
where the time goes in v4:
time: 56.9 us; the launch traced here: 56.7 us
  Pallas kernels  52.4 us (92%)
  other arithmetic  3.64 us (6%)
  between operations  0.71 us (1%)
    pallas_call x1, Pallas kernels, fused(): pl.pallas_call(kernel, out_shape=jax.ShapeDtypeStruct((8, 8, 512), f32),...  52.4 us
    div x1, other arithmetic, on_device(): return summed.reshape(1, 64, 512) / divisor  1.65 us
    add x1, other arithmetic, on_device(): line(jnp.where(used, task_amp, -1), 0) + line(task_int, 1)  1.32 us

profile of v4, /device:TPU:0, one launch (start us, length us, event | category | flops | bytes accessed | tf_op | source)
XLA Modules:
  0.0 56.7 jit_solution(14059564139541971385)
XLA Ops:
  0.0 0.0 copy-start
  0.0 0.0 copy-start.1
  0.7 0.7 %compare_select_fusion = s32[1,96]{1,0:T(1,128)S(1)} fusion(s32[1,96]{1,0:T(1,128)} %param.17, s32[]{:T(128)} %bitcast.7), kind=kLoop, calls=%fused_computation.2 | loop fusion | flops 192 | bytes 772 | tf_op jit(solution)/shard_map/jit(_where)/select_n | solution.py:473
  1.3 1.3 %pad_add_fusion.pack = s32[8,128]{1,0:T(8,128)} fusion(s32[1,8]{1,0:T(1,128)} %bitcast.10, s32[1,32]{1,0:T(1,128)} %bitcast.11, s32[1,16]{1,0:T(1,128)} %param.21, s32[1,96]{1,0:T(1,128)} %param.19, s32[1,96]{1,0:T(1,128)} %param.18, s32[1,96]{1,0:T(1,128)S(1)} %compare_select_fusion), kind=kLoop, calls=%fused_computation.1 | loop fusion | flops 5120 | bytes 5472 | tf_op jit(solution)/shard_map/add | solution.py:473
  2.7 52.4 %shard_map.121 = f32[8,8,512]{2,1,0:T(8,128)} custom-call(f32[32,64,512]{2,1,0:T(8,128)} %amp.1, f32[1,512,512]{2,1,0:T(8,128)} %integ.1, f32[8,8,512]{2,1,0:T(8,128)} %bitcast.8, s32[8,128]{1,0:T(8,128)} %pad_add_fusion.pack), custom_call_target="tpu_custom_call" | custom-call | tf_op jit(solution)/shard_map/pallas_call | solution.py:415
  55.1 0.0 copy-done
  55.1 0.0 copy-done.1
  55.1 1.7 %bitcast_divide_fusion = f32[1,64,512]{2,1,0:T(8,128)} fusion(f32[8,8,512]{2,1,0:T(8,128)} %shard_map.121, f32[512]{0:T(512)S(1)} %copy-done, f32[64]{0:T(128)S(1)} %bitcast.9), kind=kLoop, calls=%fused_computation | loop fusion | flops 65536 | bytes 264448 | tf_op jit(solution)/shard_map/div | solution.py:482
Async XLA Ops:
  0.0 55.1 %copy-start = (f32[512]{0:T(512)S(1)}, f32[512]{0:T(512)}, u32[]{:S(2)}) copy-start(f32[512]{0:T(512)} %param.16) | copy-start | bytes 6148
  0.0 55.1 %copy-start.1 = (f32[1,64]{1,0:T(1,128)S(1)}, f32[1,64]{1,0:T(1,128)}, u32[]{:S(2)}) copy-start(f32[1,64]{1,0:T(1,128)} %param.15) | copy-start | bytes 772

commit v5 on v4

--- a/solution.py
+++ b/solution.py
@@ -26,8 +26,17 @@
     amp,
     integ,
     base,
+    gap,
+    virt,
+    amp_ids,
+    int_ids,
+    res_ids,
+    count,
+    owners,
+    amp_label,
+    int_label,
+    out,
     pack,
-    out,
     a_buf,
     ib,
     shi,
@@ -94,6 +103,12 @@
         )
         loads[h].start()
 
+    pack[...] = jnp.zeros_like(pack)
+    used = iota((1, 96), 1) < count[0]
+    pack[0:1, 0:96] = jnp.where(used, amp_ids[...], -1)
+    pack[1:2, 0:96] = int_ids[...]
+    pack[2:3, 0:96] = res_ids[...]
+
     barrier = pltpu.get_barrier_semaphore()
     for dev in (right, left, twin, *along_z[1:], *along_y[1:]):
         pl.semaphore_signal(barrier, inc=1, device_id=dev, device_id_type=MESH)
@@ -203,15 +218,18 @@
     for dz, dy in beyond:
         task(dz, dy).start()
 
-    lane, row = iota((128, 128), 1), iota((128, 128), 0)
-
-    def column(values, which):
-        return jnp.sum(jnp.where(lane == which, values, 0.0), axis=1, keepdims=True)
-
-    owner = column(pack[3:4, :].astype(f32), row % 16).astype(i32)
-    sign_c = column((1 - 2 * (pack[5:6, :] & 1)).astype(f32), row // 16)
-    sign_b = (1 - 2 * (pack[4:5, :] & 1)).astype(f32)[:, :32]
+    row = iota((128, 128), 0)
+
+    def column(values, n, which):
+        lanes = iota((n, values.shape[1]), 1)
+        return jnp.sum(jnp.where(lanes == which, values, 0.0), axis=1, keepdims=True)
+
+    place = iota((128, 1), 0)
+    owner = column(owners[...].astype(f32), 128, place % 16).astype(i32)
+    sign_c = column((1 - 2 * (int_label[...] & 1)).astype(f32), 128, place // 16)
+    sign_b = (1 - 2 * (amp_label[...] & 1)).astype(f32)
     which_c = row // 16
+    gaps = column(gap[...], 64, iota((64, 1), 0)).reshape(8, 8, 1)
     local = iota((32, 128), 0) + w * 32
     real = iota((32, 128), 1) < 96
 
@@ -336,7 +354,7 @@
                 + fin[h, a, 1]
                 + fin[h, a, 2]
                 + fin[h, a, 3]
-            )
+            ) / (gaps + virt[:, cols].reshape(1, 1, 128))
 
     def events(u):
         if u == 0:
@@ -408,16 +426,18 @@
                 rs_last(h, a, d).wait_send()
 
 
-def fused(amplitudes, integrals, base, pack):
+def fused(amplitudes, integrals, base, *small):
     vmem = pl.BlockSpec(memory_space=pltpu.VMEM)
     hbm = pl.BlockSpec(memory_space=pl.ANY)
+    smem = pl.BlockSpec(memory_space=pltpu.SMEM)
     dma = pltpu.SemaphoreType.DMA
     return pl.pallas_call(
         kernel,
         out_shape=jax.ShapeDtypeStruct((8, 8, 512), f32),
-        in_specs=[hbm, hbm, vmem, vmem],
+        in_specs=[hbm, hbm, *[vmem] * 6, smem, *[vmem] * 3],
         out_specs=vmem,
         scratch_shapes=[
+            pltpu.VMEM((8, 128), i32),
             pltpu.VMEM((32, 64, 512), f32),
             pltpu.VMEM((2, 8, 512, 256), f32),
             pltpu.VMEM((8, 8, 128, 512), bf16),
@@ -446,12 +466,7 @@
         compiler_params=pltpu.CompilerParams(
             collective_id=0, has_side_effects=True, vmem_limit_bytes=60 * 2**20
         ),
-    )(amplitudes, integrals, base, pack)
-
-
-def line(values, row):
-    values = values.reshape(1, -1)
-    return jnp.pad(values, ((row, 7 - row), (0, 128 - values.shape[1])))
+    )(amplitudes, integrals, base, *small)
 
 
 def on_device(
@@ -468,18 +483,21 @@
     amp_label,
     int_label,
 ):
-    used = jnp.arange(96, dtype=i32)[None] < task_count[0]
-    pack = (
-        line(jnp.where(used, task_amp, -1), 0)
-        + line(task_int, 1)
-        + line(task_res, 2)
-        + line(res_owner, 3)
-        + line(amp_label, 4)
-        + line(int_label, 5)
+    out = fused(
+        amplitudes,
+        integrals,
+        base_residual.reshape(8, 8, 512),
+        occ_gap,
+        virt_sum.reshape(1, 512),
+        task_amp,
+        task_int,
+        task_res,
+        task_count,
+        res_owner,
+        amp_label.reshape(1, 32),
+        int_label.reshape(1, 8),
     )
-    summed = fused(amplitudes, integrals, base_residual.reshape(8, 8, 512), pack)
-    divisor = occ_gap[:, :, None] + virt_sum[None, None, :]
-    return summed.reshape(1, 64, 512) / divisor
+    return out.reshape(1, 64, 512)
 
 
 def solution(mesh):

time: 56.9 us -> 55 us (0.967)
  other arithmetic: 3.64 us -> 0 us
  local copies, waits for them, and re-layouts: 0.01 us -> 1.57 us
    div x1 -> x0, other arithmetic: 1.65 us -> none  [on_device(): return summed.reshape(1, 64, 512) / divisor]
    unnamed x4 -> x1, local copies, waits for them, and re-layouts: 0.01 us -> 1.57 us
    add x1 -> x0, other arithmetic: 1.32 us -> none  [on_device(): line(jnp.where(used, task_amp, -1), 0) + line(task_int, 1)]
    select_n x1 -> x0, other arithmetic: 0.66 us -> none  [on_device(): jnp.where(used, task_amp, -1)]
where the time goes in v5:
time: 55 us; the launch traced here: 54.8 us
  Pallas kernels  52.6 us (96%)
  local copies, waits for them, and re-layouts  1.57 us (3%)
  between operations  0.66 us (1%)
    pallas_call x1, Pallas kernels, fused(): pl.pallas_call(kernel, out_shape=jax.ShapeDtypeStruct((8, 8, 512), f32),...  52.6 us
    unnamed x1, local copies, waits for them, and re-layouts  1.57 us

profile of v5, /device:TPU:0, one launch (start us, length us, event | category | flops | bytes accessed | tf_op | source)
XLA Modules:
  0.0 54.8 jit_solution(13374885967893306261)
XLA Ops:
  0.7 52.6 %shard_map.118 = f32[8,8,512]{2,1,0:T(8,128)} custom-call(f32[32,64,512]{2,1,0:T(8,128)} %amp.1, f32[1,512,512]{2,1,0:T(8,128)} %integ.1, f32[8,8,512]{2,1,0:T(8,128)} %bitcast.6, f32[1,64]{1,0:T(1,128)} %gap.1, f32[1,512]{1,0:T(1,128)} %bitcast.7, s32[1,96]{1,0:T(1,128)} %amp_ids.1, s32[1,96]{1,0:T(1,128)} %int_ids.1, s32[1,96]{1,0:T(1,128)} %res_ids.1, ...), custom_call_target="tpu_custom_call" | custom-call | tf_op jit(solution)/shard_map/pallas_call | solution.py:434
  53.3 1.6 %copy.15 = f32[1,64,512]{2,1,0:T(8,128)} copy(f32[1,64,512]{2,1,0:T(8,128)} %bitcast.5) | data formatting | bytes 262144

commit v6 on v5

--- a/solution.py
+++ b/solution.py
@@ -268,22 +268,15 @@
     load.wait()
 
     def form(i, _):
-        @pl.when(i == 1)
+        @pl.when(i == 2)
         def _():
             got_x(0, 2)
             got_x(0, 3)
 
-        @pl.when(i == 4)
+        @pl.when(i == 5)
         def _():
             got_x(1, 0)
             got_x(1, 1)
-
-        @pl.when(i == 6)
-        def _():
-            got_x(0, 4)
-            got_x(0, 5)
-            got_q(0, 0)
-            got_q(0, 1)
 
         part = a_buf[:, pl.ds(pl.multiple_of(i * 8, 8), 8), :].reshape(256, 512)
         hi, lo = split(part)
@@ -359,28 +352,32 @@
     def events(u):
         if u == 0:
             loads[0].wait()
+            got_x(0, 4)
+            got_x(0, 5)
         if u == 1:
             twin_own_in(0).wait_recv()
+            got_q(0, 0)
+            got_q(0, 1)
+        if u == 2:
+            loads[1].wait()
             got_x(1, 2)
             got_x(1, 3)
         if u == 3:
+            twin_own_in(1).wait_recv()
+        if u == 4:
             got_q(0, 2)
+        if u == 5:
             got_twin(0, 0)
-        if u == 4:
             got_x(1, 4)
             got_x(1, 5)
-        if u == 5:
+        if u == 7:
             got_twin(0, 1)
-        if u == 6:
             got_q(1, 0)
             got_q(1, 1)
-        if u == 7:
+        if u == 9:
             got_twin(0, 2)
-        if u == 8:
+        if u == 10:
             rs_one(0)
-            loads[1].wait()
-        if u == 9:
-            twin_own_in(1).wait_recv()
             got_q(1, 2)
         if u == 11:
             got_twin(1, 0)
@@ -389,9 +386,10 @@
         if u == 15:
             got_twin(1, 2)
 
-    for u in range(16):
+    order = [(h, v) for h in range(2) for v in range(2)]
+    order += [(h, v) for h in range(2) for v in range(2, 8)]
+    for u, (h, v) in enumerate(order):
         events(u)
-        h, v = u // 8, u % 8
         c = 2 * ((x + (0, 3, 1, 2)[v // 2]) % 4) + (1 - s if v % 2 else s)
         ihi, ilo = split(ib[h, c])
         for r in (slice(0, 4), slice(4, 8)):

time: 55 us -> 53.9 us (0.980)
  Pallas kernels: 52.6 us -> 51.5 us
    pallas_call x1, Pallas kernels: 52.6 us -> 51.5 us  [fused(): pl.pallas_call(kernel, out_shape=jax.ShapeDtypeStruct((8, 8, 512), f32),...]
where the time goes in v6:
time: 53.9 us; the launch traced here: 53.8 us
  Pallas kernels  51.5 us (96%)
  local copies, waits for them, and re-layouts  1.57 us (3%)
  between operations  0.66 us (1%)
    pallas_call x1, Pallas kernels, fused(): pl.pallas_call(kernel, out_shape=jax.ShapeDtypeStruct((8, 8, 512), f32),...  51.5 us
    unnamed x1, local copies, waits for them, and re-layouts  1.57 us

profile of v6, /device:TPU:0, one launch (start us, length us, event | category | flops | bytes accessed | tf_op | source)
XLA Modules:
  0.0 53.8 jit_solution(3339000595653616623)
XLA Ops:
  0.7 51.5 %shard_map.118 = f32[8,8,512]{2,1,0:T(8,128)} custom-call(f32[32,64,512]{2,1,0:T(8,128)} %amp.1, f32[1,512,512]{2,1,0:T(8,128)} %integ.1, f32[8,8,512]{2,1,0:T(8,128)} %bitcast.6, f32[1,64]{1,0:T(1,128)} %gap.1, f32[1,512]{1,0:T(1,128)} %bitcast.7, s32[1,96]{1,0:T(1,128)} %amp_ids.1, s32[1,96]{1,0:T(1,128)} %int_ids.1, s32[1,96]{1,0:T(1,128)} %res_ids.1, ...), custom_call_target="tpu_custom_call" | custom-call | tf_op jit(solution)/shard_map/pallas_call | solution.py:432
  52.2 1.6 %copy.15 = f32[1,64,512]{2,1,0:T(8,128)} copy(f32[1,64,512]{2,1,0:T(8,128)} %bitcast.5) | data formatting | bytes 262144

commit v7 on v6

--- a/solution.py
+++ b/solution.py
@@ -268,12 +268,12 @@
     load.wait()
 
     def form(i, _):
-        @pl.when(i == 2)
+        @pl.when(i == 4)
         def _():
             got_x(0, 2)
             got_x(0, 3)
 
-        @pl.when(i == 5)
+        @pl.when(i == 7)
         def _():
             got_x(1, 0)
             got_x(1, 1)
@@ -352,42 +352,44 @@
     def events(u):
         if u == 0:
             loads[0].wait()
+        if u == 1:
+            twin_own_in(0).wait_recv()
             got_x(0, 4)
             got_x(0, 5)
-        if u == 1:
-            twin_own_in(0).wait_recv()
+        if u == 2:
+            loads[1].wait()
             got_q(0, 0)
             got_q(0, 1)
-        if u == 2:
-            loads[1].wait()
+        if u == 3:
+            twin_own_in(1).wait_recv()
             got_x(1, 2)
             got_x(1, 3)
-        if u == 3:
-            twin_own_in(1).wait_recv()
-        if u == 4:
+        if u == 5:
             got_q(0, 2)
-        if u == 5:
+        if u == 6:
             got_twin(0, 0)
             got_x(1, 4)
             got_x(1, 5)
         if u == 7:
             got_twin(0, 1)
+        if u == 8:
             got_q(1, 0)
             got_q(1, 1)
         if u == 9:
             got_twin(0, 2)
         if u == 10:
             rs_one(0)
+        if u == 11:
             got_q(1, 2)
-        if u == 11:
-            got_twin(1, 0)
         if u == 13:
             got_twin(1, 1)
         if u == 15:
             got_twin(1, 2)
+        if u == 12:
+            got_twin(1, 0)
 
     order = [(h, v) for h in range(2) for v in range(2)]
-    order += [(h, v) for h in range(2) for v in range(2, 8)]
+    order += [(h, v) for h in range(2) for v in (2, 4, 3, 5, 6, 7)]
     for u, (h, v) in enumerate(order):
         events(u)
         c = 2 * ((x + (0, 3, 1, 2)[v // 2]) % 4) + (1 - s if v % 2 else s)

time: 53.9 us -> 53.1 us (0.985)
  Pallas kernels: 51.5 us -> 50.7 us
    pallas_call x1, Pallas kernels: 51.5 us -> 50.7 us  [fused(): pl.pallas_call(kernel, out_shape=jax.ShapeDtypeStruct((8, 8, 512), f32),...]
where the time goes in v7:
time: 53.1 us; the launch traced here: 52.9 us
  Pallas kernels  50.7 us (95%)
  local copies, waits for them, and re-layouts  1.57 us (3%)
  between operations  0.66 us (1%)
    pallas_call x1, Pallas kernels, fused(): pl.pallas_call(kernel, out_shape=jax.ShapeDtypeStruct((8, 8, 512), f32),...  50.7 us
    unnamed x1, local copies, waits for them, and re-layouts  1.57 us

profile of v7, /device:TPU:0, one launch (start us, length us, event | category | flops | bytes accessed | tf_op | source)
XLA Modules:
  0.0 52.9 jit_solution(1885638587948029514)
XLA Ops:
  0.7 50.7 %shard_map.118 = f32[8,8,512]{2,1,0:T(8,128)} custom-call(f32[32,64,512]{2,1,0:T(8,128)} %amp.1, f32[1,512,512]{2,1,0:T(8,128)} %integ.1, f32[8,8,512]{2,1,0:T(8,128)} %bitcast.6, f32[1,64]{1,0:T(1,128)} %gap.1, f32[1,512]{1,0:T(1,128)} %bitcast.7, s32[1,96]{1,0:T(1,128)} %amp_ids.1, s32[1,96]{1,0:T(1,128)} %int_ids.1, s32[1,96]{1,0:T(1,128)} %res_ids.1, ...), custom_call_target="tpu_custom_call" | custom-call | tf_op jit(solution)/shard_map/pallas_call | solution.py:434
  51.4 1.6 %copy.15 = f32[1,64,512]{2,1,0:T(8,128)} copy(f32[1,64,512]{2,1,0:T(8,128)} %bitcast.5) | data formatting | bytes 262144

commit v8 on v7

--- a/solution.py
+++ b/solution.py
@@ -92,6 +92,9 @@
             device_id_type=MESH,
         )
 
+    barrier = pltpu.get_barrier_semaphore()
+    for dev in (right, left, twin, *along_z[1:], *along_y[1:]):
+        pl.semaphore_signal(barrier, inc=1, device_id=dev, device_id_type=MESH)
     load = pltpu.make_async_copy(amp, a_buf, a_sem)
     load.start()
     loads = []
@@ -108,10 +111,6 @@
     pack[0:1, 0:96] = jnp.where(used, amp_ids[...], -1)
     pack[1:2, 0:96] = int_ids[...]
     pack[2:3, 0:96] = res_ids[...]
-
-    barrier = pltpu.get_barrier_semaphore()
-    for dev in (right, left, twin, *along_z[1:], *along_y[1:]):
-        pl.semaphore_signal(barrier, inc=1, device_id=dev, device_id_type=MESH)
     pl.semaphore_wait(barrier, 9)
 
     for d in range(1, 4):
@@ -234,12 +233,12 @@
     real = iota((32, 128), 1) < 96
 
     keep.wait()
+    for dz, dy in beside + beyond:
+        task(dz, dy, 1).wait_recv()
     got_x(0, 0)
     got_x(0, 1)
     for k in (2, 3):
         x_own(1, k).start()
-    for dz, dy in beside + beyond:
-        task(dz, dy, 1).wait_recv()
     hits, picks = [], []
     for v in range(16):
         names = tb[v // 4, v % 4]

time: 53.1 us -> 53 us (level)
  no operation moved by 1% of the time
where the time goes in v8:
time: 53 us; the launch traced here: 52.9 us
  Pallas kernels  50.7 us (96%)
  local copies, waits for them, and re-layouts  1.57 us (3%)
  between operations  0.66 us (1%)
    pallas_call x1, Pallas kernels, fused(): pl.pallas_call(kernel, out_shape=jax.ShapeDtypeStruct((8, 8, 512), f32),...  50.7 us
    unnamed x1, local copies, waits for them, and re-layouts  1.57 us

profile of v8, /device:TPU:0, one launch (start us, length us, event | category | flops | bytes accessed | tf_op | source)
XLA Modules:
  0.0 52.9 jit_solution(2399744782348241445)
XLA Ops:
  0.7 50.7 %shard_map.118 = f32[8,8,512]{2,1,0:T(8,128)} custom-call(f32[32,64,512]{2,1,0:T(8,128)} %amp.1, f32[1,512,512]{2,1,0:T(8,128)} %integ.1, f32[8,8,512]{2,1,0:T(8,128)} %bitcast.6, f32[1,64]{1,0:T(1,128)} %gap.1, f32[1,512]{1,0:T(1,128)} %bitcast.7, s32[1,96]{1,0:T(1,128)} %amp_ids.1, s32[1,96]{1,0:T(1,128)} %int_ids.1, s32[1,96]{1,0:T(1,128)} %res_ids.1, ...), custom_call_target="tpu_custom_call" | custom-call | tf_op jit(solution)/shard_map/pallas_call | solution.py:433
  51.3 1.6 %copy.15 = f32[1,64,512]{2,1,0:T(8,128)} copy(f32[1,64,512]{2,1,0:T(8,128)} %bitcast.5) | data formatting | bytes 262144
